TPU v7x, 128 devices: a whole 4x4x4 slice. The times are simulated.
128 devices in a mesh: dom: 16 (over y, z), sub: 8 (over x, core).
Axes of the slice: x: 4, y: 4, z: 4, core: 2. Of those that a mesh axis runs over, the one named last changes fastest.
Arguments:
- pos_vel: float32 [32768, 6, 128], P(('dom', 'sub')), may hold values from -6 to 6
- entropy: float32 [32768, 128], P(('dom', 'sub')), may hold values from 0.5 to 4
- masses: float32 [32768, 128], P(('dom', 'sub')), may hold values from 0.5 to 2
- destination: int32 [32768], P(('dom', 'sub')), may hold values from 0 to 127, as said below
- ghost_send: int32 [2, 16384], P(None, ('dom', 'sub')), may hold values from 0 to 255
- pair_list: int32 [2, 32768, 2], P(None, ('dom', 'sub')), may hold values from 0 to 383
Outputs:
- final_state: float32 [32768, 6, 128], P(('dom', 'sub'))
- density: float32 [32768, 128], P(('dom', 'sub'))
Inputs may be any that keep to these rules, and one draw needn't show every extreme that they name: `destination`: each device sends exactly 128 of its blocks to other devices and keeps the rest, so it also receives exactly 128. The number of blocks that device s sends to device (s + k) modulo the device count depends only on k, is at most 2, and equals 2 for some k.
All inputs are finite; a program needn't handle non-finite values.
Results may differ from a plain program's by a relative error of at most 0.0001.
Values sent between devices are 32-bit elements; how exact they have to be, the bound alone decides.
A program may use at most 64 MiB of HBM per device.

v0:
```python
import jax
import jax.numpy as jnp
from jax import lax
from jax.sharding import PartitionSpec as P

MOST = 2


time_step = 0.25
group_rows = 32


def with_halo(array, sides, width):
    for axis, dim in sides:
        devices, length = (lax.axis_size(axis), array.shape[dim])
        up = [(i, (i + 1) % devices) for i in range(devices - 1)]
        down = [(j, i) for i, j in up]
        last = lax.slice_in_dim(array, length - width, length, axis=dim)
        leading = lax.slice_in_dim(array, 0, width, axis=dim)
        before = lax.ppermute(last, axis, up)
        after = lax.ppermute(leading, axis, down)
        array = jnp.concatenate([before, array, after], axis=dim)
    return array


def prefix(part, axis, combine, identity):
    place = lax.axis_index(axis)
    gathered = lax.all_gather(part, axis)
    state = jnp.zeros_like(part) + jnp.asarray(identity, part.dtype)

    def one(lap, state):
        return combine(state, lax.dynamic_index_in_dim(gathered, lap, 0, False))

    return lax.fori_loop(0, place, one, state)


def interact(near_block, far_block, near_press, far_press):
    diff_x = near_block[:, 0, :, None] - far_block[:, 0, None, :]
    diff_y = near_block[:, 1, :, None] - far_block[:, 1, None, :]
    diff_z = near_block[:, 2, :, None] - far_block[:, 2, None, :]
    kernel = jnp.exp(-0.5 * (diff_x * diff_x + diff_y * diff_y + diff_z * diff_z))
    near_mass = near_block[:, 3, :, None]
    far_mass = far_block[:, 3, None, :]
    if near_press is None:
        to_self = jnp.sum(kernel * far_mass, axis=2)[:, None, :]
        to_other = jnp.sum(kernel * near_mass, axis=1)[:, None, :]
        return (to_self, to_other)
    coupling = kernel * near_mass * far_mass * (near_press[:, :, None] + far_press[:, None, :])
    to_self = jnp.stack(
        [
            jnp.sum(coupling * diff_x, axis=2),
            jnp.sum(coupling * diff_y, axis=2),
            jnp.sum(coupling * diff_z, axis=2),
        ],
        axis=1,
    )
    to_other = -jnp.stack(
        [
            jnp.sum(coupling * diff_x, axis=1),
            jnp.sum(coupling * diff_y, axis=1),
            jnp.sum(coupling * diff_z, axis=1),
        ],
        axis=1,
    )
    return (to_self, to_other)


def pair_pass(combined, listed, pressure):
    local_count = listed.shape[0]
    columns = listed.shape[1]
    rows_out = 1 if pressure is None else 3
    totals = jnp.zeros((combined.shape[0], rows_out, combined.shape[2]), jnp.float32)

    def one_group(group_index, totals):
        first_row = group_index * group_rows
        leaf_block = lax.dynamic_slice_in_dim(combined, first_row, group_rows, 0)
        partners = lax.dynamic_slice_in_dim(listed, first_row, group_rows, 0)
        near_press = (
            None
            if pressure is None
            else lax.dynamic_slice_in_dim(pressure, first_row, group_rows, 0)
        )
        own_sum, unused = interact(leaf_block, leaf_block, near_press, near_press)
        for column in range(columns):
            target = partners[:, column]
            partner = combined[target]
            far_press = None if pressure is None else pressure[target]
            to_self, to_other = interact(leaf_block, partner, near_press, far_press)
            own_sum = own_sum + to_self
            totals = totals.at[target].add(to_other)
        current = lax.dynamic_slice_in_dim(totals, first_row, group_rows, 0)
        return lax.dynamic_update_slice_in_dim(totals, current + own_sum, first_row, 0)

    return lax.fori_loop(0, local_count // group_rows, one_group, totals)


def outward(picked):
    half_rows = picked.shape[0] // 2
    extended = with_halo(picked, (("dom", 0),), half_rows)
    return jnp.concatenate([extended[:half_rows], extended[3 * half_rows :]], 0)


def inward(partials, send_rows, local_count):
    half_rows = send_rows.shape[0] // 2
    extended = with_halo(partials[local_count:], (("dom", 0),), half_rows)
    incoming = jnp.concatenate([extended[:half_rows], extended[3 * half_rows :]], 0)
    return partials[:local_count].at[send_rows].add(incoming)


def add_counts(earlier_sum, later_sum):
    return earlier_sum + later_sum


def shards(pos_vel, entropy, masses, destination, ghost_send, pair_list):
    dev_count = lax.axis_size(("dom", "sub"))
    my_index = lax.axis_index(("dom", "sub"))
    local_count = pos_vel.shape[0]
    block_size = pos_vel.shape[2]
    packed = jnp.concatenate([pos_vel, entropy[:, None], masses[:, None]], 1)
    staying = destination == my_index
    targets = jnp.arange(dev_count, dtype=jnp.int32)
    routed = (
        (destination[:, None] == targets[None, :]) & jnp.logical_not(staying)[:, None]
    ).astype(jnp.int32)
    counts = jnp.sum(routed, 0)
    earlier = jnp.cumsum(routed, 0) - routed
    rank_out = jnp.sum(earlier * routed, 1)
    out_slot = jnp.where(staying, dev_count * MOST, destination * MOST + rank_out)
    outbox = (
        jnp.zeros((dev_count * MOST, 8, block_size), jnp.float32)
        .at[out_slot]
        .set(packed, mode="drop")
    )
    offsets = prefix(counts, ("dom", "sub"), add_counts, jnp.zeros_like(counts))
    labels = jnp.sum(offsets[None, :] * routed, 1) + rank_out + 1
    slot_tags = jnp.zeros((dev_count * MOST,), jnp.int32).at[out_slot].set(labels, mode="drop")
    arrived, arrived_tags = (
        lax.all_to_all(
            outbox.reshape(dev_count, MOST, 8, block_size),
            ("dom", "sub"),
            split_axis=0,
            concat_axis=0,
            tiled=True,
        ),
        lax.all_to_all(
            slot_tags.reshape(dev_count, MOST),
            ("dom", "sub"),
            split_axis=0,
            concat_axis=0,
            tiled=True,
        ),
    )
    arrived = arrived.reshape(dev_count * MOST, 8, block_size)
    arrived_tags = arrived_tags.reshape(dev_count * MOST)
    present = arrived_tags > 0
    slot_in = arrived_tags - 1
    in_slot = jnp.where(present, local_count - dev_count + slot_in, local_count)
    keep_slot = jnp.where(staying, jnp.cumsum(staying.astype(jnp.int32)) - 1, local_count)
    rehomed = (
        jnp.zeros((local_count, 8, block_size), jnp.float32).at[keep_slot].set(packed, mode="drop")
    )
    rehomed = rehomed.at[in_slot].set(arrived, mode="drop")
    particle = rehomed[:, 0:6]
    entropy_now = rehomed[:, 6]
    mass_now = rehomed[:, 7]
    density = jnp.zeros((local_count, 1, block_size), jnp.float32)
    for section_index in range(ghost_send.shape[0]):
        send_rows = ghost_send[section_index]
        listed = pair_list[section_index]
        physical = jnp.concatenate([particle[:, 0:3], mass_now[:, None]], 1)
        ghosts = outward(physical[send_rows])
        combined = jnp.concatenate([physical, ghosts], 0)
        partial_rho = pair_pass(combined, listed, None)
        density = inward(partial_rho, send_rows, local_count)
        pressure = entropy_now * density[:, 0] ** (-1.0 / 3.0)
        ghost_press = outward(pressure[send_rows][:, None])[:, 0]
        press_all = jnp.concatenate([pressure, ghost_press], 0)
        partial_force = pair_pass(combined, listed, press_all)
        force_sum = inward(partial_force, send_rows, local_count)
        velocity = particle[:, 3:6] + time_step * force_sum / mass_now[:, None]
        position = particle[:, 0:3] + time_step * velocity
        particle = jnp.concatenate([position, velocity], 1)
    return (particle, density[:, 0])


def solution(mesh):
    in_specs = (
        P(("dom", "sub"), None, None),
        P(("dom", "sub"), None),
        P(("dom", "sub"), None),
        P(("dom", "sub")),
        P(None, ("dom", "sub")),
        P(None, ("dom", "sub"), None),
    )
    out_specs = (P(("dom", "sub"), None, None), P(("dom", "sub"), None))
    return jax.shard_map(shards, mesh=mesh, in_specs=in_specs, out_specs=out_specs, check_vma=False)
```

profile of v0, /device:TPU:8, one launch (start us, length us, event | category | flops | bytes accessed | tf_op | source)
XLA Modules:
  0.0 707.5 jit_solution(3725005262953901687)
XLA Ops:
  2.3 32.8 %all-gather.1 = s32[128,1,128]{2,1,0:T(1,128)S(1)} all-gather(s32[1,1,128]{2,1,0:T(1,128)S(1)} %bitcast.439), channel_id=2, replica_groups=mesh['dom'=16,'sub'=8] {'dom','sub'}, dimensions={0}, use_global_device_ids=true | all-gather | bytes 66048 | tf_op jit(solution)/shard_map/all_gather | solution.py:28
  40.7 10.4 %all-to-all-start = ((s32[128,1,2]{2,1,0:T(1,128)}), s32[128,1,2]{2,1,0:T(1,128)S(1)}, u32[]{:S(2)}, u32[]{:S(2)}) async-start(s32[128,1,2]{2,1,0:T(1,128)} %bitcast.104), calls=%async_computation | async-start | bytes 131072 | tf_op jit(solution)/shard_map/all_to_all | solution.py:145
  52.8 27.1 %scatter_fusion.9 = f32[256,8,128]{2,1,0:T(8,128)} fusion(f32[256,8,128]{2,1,0:T(8,128)} %broadcast.264.clone.1, s32[256]{0:T(256)S(1)} %get-tuple-element.613, f32[256,8,128]{2,1,0:T(8,128)S(1)} %copy.50), kind=kCustom, calls=%fused_computation.26 | custom fusion | bytes 3146752 | tf_op jit(solution)/shard_map/scatter | solution.py:132
  97.6 10.5 %all-to-all-done.1 = f32[128,2,8,128]{3,2,1,0:T(8,128)S(1)} async-done(((f32[128,2,8,128]{3,2,1,0:T(8,128)}), f32[128,2,8,128]{3,2,1,0:T(8,128)S(1)}, u32[]{:S(2)}, u32[]{:S(2)}) %all-to-all-start.1) | async-done | bytes 1048608 | tf_op jit(solution)/shard_map/all_to_all | solution.py:138
  129.7 69.8 %while.63 = (s32[]{:T(128)}, f32[384,1,128]{2,0,1:T(8,128)S(1)}, s32[256,2]{0,1:T(2,128)S(1)}, f32[384,4,128]{2,1,0:T(4,128)S(1)}, s32[]{:T(128)}, /*index=5*/s3...) while((s32[]{:T(128)}, f32[384,1,128]{2,0,1:T(8,128)S(1)}, ...), condition=%wide.region_21.22_spmd, body=%wide.region_13.21_spmd.sunk | while | flops 19400908 | bytes 1910784 | solution.py:94
  221.5 133.0 %while.64 = (s32[]{:T(128)}, f32[384,3,128]{2,1,0:T(4,128)S(1)}, s32[256,2]{0,1:T(2,128)S(1)}, f32[384,4,128]{2,1,0:T(4,128)S(1)}, f32[384,128]{1,0:T(8,128)S(1)...) while((s32[]{:T(128)}, f32[384,3,128]{2,1,0:T(4,128)S(1)}, ...), condition=%wide.region_41.42_spmd, body=%wide.region_23.41_spmd.sunk | while | flops 33179852 | bytes 2222348 | solution.py:94
  224.2 10.4 %fusion.146 = (f32[32,128]{1,0:T(8,128)S(1)}, f32[32,128]{1,0:T(8,128)S(1)}, f32[32,128]{1,0:T(8,128)S(1)}, f32[32,128]{1,0:T(8,128)S(1)}, f32[32,128]{1,0:T(8,1...) fusion(f32[32,128]{1,0:T(8,128)S(1)} %bitcast.387, ...), kind=kLoop, calls=%fused_computation.100.clone.1 | loop fusion | flops 32968704 | bytes 491520 | tf_op jit(solution)/shard_map/while/body/eval_jaxpr/reduce_sum | solution.py:51
  240.9 10.4 %fusion.146 = (f32[32,128]{1,0:T(8,128)S(1)}, f32[32,128]{1,0:T(8,128)S(1)}, f32[32,128]{1,0:T(8,128)S(1)}, f32[32,128]{1,0:T(8,128)S(1)}, f32[32,128]{1,0:T(8,1...) fusion(f32[32,128]{1,0:T(8,128)S(1)} %bitcast.387, ...), kind=kLoop, calls=%fused_computation.100.clone.1 | loop fusion | flops 32968704 | bytes 491520 | tf_op jit(solution)/shard_map/while/body/eval_jaxpr/reduce_sum | solution.py:51
  257.5 10.4 %fusion.146 = (f32[32,128]{1,0:T(8,128)S(1)}, f32[32,128]{1,0:T(8,128)S(1)}, f32[32,128]{1,0:T(8,128)S(1)}, f32[32,128]{1,0:T(8,128)S(1)}, f32[32,128]{1,0:T(8,1...) fusion(f32[32,128]{1,0:T(8,128)S(1)} %bitcast.387, ...), kind=kLoop, calls=%fused_computation.100.clone.1 | loop fusion | flops 32968704 | bytes 491520 | tf_op jit(solution)/shard_map/while/body/eval_jaxpr/reduce_sum | solution.py:51
  274.1 10.4 %fusion.146 = (f32[32,128]{1,0:T(8,128)S(1)}, f32[32,128]{1,0:T(8,128)S(1)}, f32[32,128]{1,0:T(8,128)S(1)}, f32[32,128]{1,0:T(8,128)S(1)}, f32[32,128]{1,0:T(8,1...) fusion(f32[32,128]{1,0:T(8,128)S(1)} %bitcast.387, ...), kind=kLoop, calls=%fused_computation.100.clone.1 | loop fusion | flops 32968704 | bytes 491520 | tf_op jit(solution)/shard_map/while/body/eval_jaxpr/reduce_sum | solution.py:51
  290.7 10.4 %fusion.146 = (f32[32,128]{1,0:T(8,128)S(1)}, f32[32,128]{1,0:T(8,128)S(1)}, f32[32,128]{1,0:T(8,128)S(1)}, f32[32,128]{1,0:T(8,128)S(1)}, f32[32,128]{1,0:T(8,1...) fusion(f32[32,128]{1,0:T(8,128)S(1)} %bitcast.387, ...), kind=kLoop, calls=%fused_computation.100.clone.1 | loop fusion | flops 32968704 | bytes 491520 | tf_op jit(solution)/shard_map/while/body/eval_jaxpr/reduce_sum | solution.py:51
  307.3 10.4 %fusion.146 = (f32[32,128]{1,0:T(8,128)S(1)}, f32[32,128]{1,0:T(8,128)S(1)}, f32[32,128]{1,0:T(8,128)S(1)}, f32[32,128]{1,0:T(8,128)S(1)}, f32[32,128]{1,0:T(8,1...) fusion(f32[32,128]{1,0:T(8,128)S(1)} %bitcast.387, ...), kind=kLoop, calls=%fused_computation.100.clone.1 | loop fusion | flops 32968704 | bytes 491520 | tf_op jit(solution)/shard_map/while/body/eval_jaxpr/reduce_sum | solution.py:51
  324.0 10.4 %fusion.146 = (f32[32,128]{1,0:T(8,128)S(1)}, f32[32,128]{1,0:T(8,128)S(1)}, f32[32,128]{1,0:T(8,128)S(1)}, f32[32,128]{1,0:T(8,128)S(1)}, f32[32,128]{1,0:T(8,1...) fusion(f32[32,128]{1,0:T(8,128)S(1)} %bitcast.387, ...), kind=kLoop, calls=%fused_computation.100.clone.1 | loop fusion | flops 32968704 | bytes 491520 | tf_op jit(solution)/shard_map/while/body/eval_jaxpr/reduce_sum | solution.py:51
  383.6 75.2 %while.65 = (s32[]{:T(128)}, f32[384,1,128]{2,0,1:T(8,128)S(1)}, s32[256,2]{0,1:T(2,128)}, f32[384,4,128]{2,1,0:T(4,128)S(1)}, s32[]{:T(128)}, /*index=5*/s32[]{...) while((s32[]{:T(128)}, f32[384,1,128]{2,0,1:T(8,128)S(1)}, s32[256,2]{0,1:T(2,128)}, ...), condition=%wide.region_51.52_spmd, body=%wide.region_43.51_spmd.sunk | while | flops 19400908 | bytes 1910784 | solution.py:94
  480.8 199.1 %while.66 = (s32[]{:T(128)}, f32[384,3,128]{2,1,0:T(4,128)S(1)}, s32[256,2]{0,1:T(2,128)}, f32[384,4,128]{2,1,0:T(4,128)S(1)}, f32[384,128]{1,0:T(8,128)S(1)}, /...) while((s32[]{:T(128)}, f32[384,3,128]{2,1,0:T(4,128)S(1)}, ...), condition=%wide.region_71.72_spmd, body=%wide.region_53.71_spmd.sunk | while | flops 33179852 | bytes 2223428 | solution.py:94
  487.7 12.7 %fusion.154 = (f32[32,128]{1,0:T(8,128)S(1)}, f32[32,128]{1,0:T(8,128)}, f32[32,128]{1,0:T(8,128)}, f32[32,128]{1,0:T(8,128)}, f32[32,128]{1,0:T(8,128)}, /*inde...) fusion(f32[32,128]{1,0:T(8,128)} %bitcast.391, ...), kind=kLoop, calls=%fused_computation.191.clone.1 | loop fusion | flops 32968704 | bytes 491520 | tf_op jit(solution)/shard_map/while/body/eval_jaxpr/reduce_sum | solution.py:51
  512.6 12.7 %fusion.154 = (f32[32,128]{1,0:T(8,128)S(1)}, f32[32,128]{1,0:T(8,128)}, f32[32,128]{1,0:T(8,128)}, f32[32,128]{1,0:T(8,128)}, f32[32,128]{1,0:T(8,128)}, /*inde...) fusion(f32[32,128]{1,0:T(8,128)} %bitcast.391, ...), kind=kLoop, calls=%fused_computation.191.clone.1 | loop fusion | flops 32968704 | bytes 491520 | tf_op jit(solution)/shard_map/while/body/eval_jaxpr/reduce_sum | solution.py:51
  537.5 12.7 %fusion.154 = (f32[32,128]{1,0:T(8,128)S(1)}, f32[32,128]{1,0:T(8,128)}, f32[32,128]{1,0:T(8,128)}, f32[32,128]{1,0:T(8,128)}, f32[32,128]{1,0:T(8,128)}, /*inde...) fusion(f32[32,128]{1,0:T(8,128)} %bitcast.391, ...), kind=kLoop, calls=%fused_computation.191.clone.1 | loop fusion | flops 32968704 | bytes 491520 | tf_op jit(solution)/shard_map/while/body/eval_jaxpr/reduce_sum | solution.py:51
  562.4 12.7 %fusion.154 = (f32[32,128]{1,0:T(8,128)S(1)}, f32[32,128]{1,0:T(8,128)}, f32[32,128]{1,0:T(8,128)}, f32[32,128]{1,0:T(8,128)}, f32[32,128]{1,0:T(8,128)}, /*inde...) fusion(f32[32,128]{1,0:T(8,128)} %bitcast.391, ...), kind=kLoop, calls=%fused_computation.191.clone.1 | loop fusion | flops 32968704 | bytes 491520 | tf_op jit(solution)/shard_map/while/body/eval_jaxpr/reduce_sum | solution.py:51
  587.2 12.7 %fusion.154 = (f32[32,128]{1,0:T(8,128)S(1)}, f32[32,128]{1,0:T(8,128)}, f32[32,128]{1,0:T(8,128)}, f32[32,128]{1,0:T(8,128)}, f32[32,128]{1,0:T(8,128)}, /*inde...) fusion(f32[32,128]{1,0:T(8,128)} %bitcast.391, ...), kind=kLoop, calls=%fused_computation.191.clone.1 | loop fusion | flops 32968704 | bytes 491520 | tf_op jit(solution)/shard_map/while/body/eval_jaxpr/reduce_sum | solution.py:51
  612.1 12.7 %fusion.154 = (f32[32,128]{1,0:T(8,128)S(1)}, f32[32,128]{1,0:T(8,128)}, f32[32,128]{1,0:T(8,128)}, f32[32,128]{1,0:T(8,128)}, f32[32,128]{1,0:T(8,128)}, /*inde...) fusion(f32[32,128]{1,0:T(8,128)} %bitcast.391, ...), kind=kLoop, calls=%fused_computation.191.clone.1 | loop fusion | flops 32968704 | bytes 491520 | tf_op jit(solution)/shard_map/while/body/eval_jaxpr/reduce_sum | solution.py:51
  637.0 12.7 %fusion.154 = (f32[32,128]{1,0:T(8,128)S(1)}, f32[32,128]{1,0:T(8,128)}, f32[32,128]{1,0:T(8,128)}, f32[32,128]{1,0:T(8,128)}, f32[32,128]{1,0:T(8,128)}, /*inde...) fusion(f32[32,128]{1,0:T(8,128)} %bitcast.391, ...), kind=kLoop, calls=%fused_computation.191.clone.1 | loop fusion | flops 32968704 | bytes 491520 | tf_op jit(solution)/shard_map/while/body/eval_jaxpr/reduce_sum | solution.py:51
  661.9 12.7 %fusion.154 = (f32[32,128]{1,0:T(8,128)S(1)}, f32[32,128]{1,0:T(8,128)}, f32[32,128]{1,0:T(8,128)}, f32[32,128]{1,0:T(8,128)}, f32[32,128]{1,0:T(8,128)}, /*inde...) fusion(f32[32,128]{1,0:T(8,128)} %bitcast.391, ...), kind=kLoop, calls=%fused_computation.191.clone.1 | loop fusion | flops 32968704 | bytes 491520 | tf_op jit(solution)/shard_map/while/body/eval_jaxpr/reduce_sum | solution.py:51
  691.1 13.7 %scatter_fusion.12 = f32[256,3,128]{2,1,0:T(4,128)} fusion(f32[256,3,128]{2,1,0:T(4,128)} %slice.596, s32[128]{0:T(128)S(1)} %copy-done.10, f32[128,3,128]{2,1,0:T(4,128)S(1)} %pad_maximum_fusion.7), kind=kCustom, calls=%fused_computation.31 | custom fusion | flops 49152 | bytes 590336 | tf_op jit(solution)/shard_map/scatter-add | solution.py:107
  (712 shorter events, 435.4 us)
Async XLA Ops:
  0.6 37.5 %copy-start.8 = (s32[256]{0:T(256)S(1)}, s32[256]{0:T(256)}, u32[]{:S(2)}) copy-start(s32[256]{0:T(256)} %param.19) | copy-start | bytes 3076
  0.6 50.4 %copy-start.4 = (f32[256,128]{1,0:T(8,128)S(1)}, f32[256,128]{1,0:T(8,128)}, u32[]{:S(2)}) copy-start(f32[256,128]{1,0:T(8,128)} %param.18) | copy-start | bytes 393220
  0.7 50.4 %copy-start.5 = (f32[256,128]{1,0:T(8,128)S(1)}, f32[256,128]{1,0:T(8,128)}, u32[]{:S(2)}) copy-start(f32[256,128]{1,0:T(8,128)} %param.17) | copy-start | bytes 393220
  0.7 50.4 %copy-start.2 = (f32[256,6,128]{2,0,1:T(8,128)S(1)}, f32[256,6,128]{2,0,1:T(8,128)}, u32[]{:S(2)}) copy-start(f32[256,6,128]{2,0,1:T(8,128)} %param.16) | copy-start | bytes 2359300
  40.7 39.3 %all-to-all-start = ((s32[128,1,2]{2,1,0:T(1,128)}), s32[128,1,2]{2,1,0:T(1,128)S(1)}, u32[]{:S(2)}, u32[]{:S(2)}) async-start(s32[128,1,2]{2,1,0:T(1,128)} %bitcast.104), calls=%async_computation | async-start | bytes 131072 | tf_op jit(solution)/shard_map/all_to_all | solution.py:145
  79.9 28.2 %all-to-all-start.1 = ((f32[128,2,8,128]{3,2,1,0:T(8,128)}), f32[128,2,8,128]{3,2,1,0:T(8,128)S(1)}, u32[]{:S(2)}, u32[]{:S(2)}) async-start(f32[128,2,8,128]{3,2,1,0:T(8,128)} %bitcast.106), calls=%async_computation.1 | async-start | bytes 2097152 | tf_op jit(solution)/shard_map/all_to_all | solution.py:138
  97.2 112.2 %copy-start.11 = (s32[128]{0:T(128)}, s32[128]{0:T(128)S(1)}, u32[]{:S(2)}) copy-start(s32[128]{0:T(128)S(1)} %get-tuple-element.611) | copy-start | bytes 1540
  116.8 6.9 collective-permute-start.1
  120.2 9.1 %collective-permute-start = (f32[64,4,128]{2,1,0:T(4,128)S(1)}, f32[64,4,128]{2,1,0:T(4,128)S(1)}, u32[]{:S(2)}, u32[]{:S(2)}) collective-permute-start(f32[64,4,128]{2,1,0:T(4,128)S(1)} %get-tuple-element.598), channel_id=1, source_target_pairs={{0,8},{8,16},{16,24},{24,32},{32,40},{40,48},{48,56},{56,64},{64,7... | collective-permute-start | bytes 393224 | tf_op jit(solution)/shard_map/ppermute | solution.py:20
  199.6 5.9 collective-permute-start.3
  201.5 7.9 %collective-permute-start.2 = (f32[64,1,128]{2,0,1:T(8,128)S(1)}, f32[64,1,128]{2,0,1:T(8,128)S(1)}, u32[]{:S(2)}, u32[]{:S(2)}) collective-permute-start(f32[64,1,128]{2,0,1:T(8,128)S(1)} %get-tuple-element.602), channel_id=1, source_target_pairs={{0,8},{8,16},{16,24},{24,32},{32,40},{40,48},{48,56},{56,64},{64,7... | collective-permute-start | bytes 98312 | tf_op jit(solution)/shard_map/ppermute | solution.py:20
  211.6 6.0 collective-permute-start.5
  213.5 7.9 %collective-permute-start.4 = (f32[64,1,128]{2,0,1:T(8,128)S(1)}, f32[64,1,128]{2,0,1:T(8,128)S(1)}, u32[]{:S(2)}, u32[]{:S(2)}) collective-permute-start(f32[64,1,128]{2,0,1:T(8,128)S(1)} %get-tuple-element.606), channel_id=1, source_target_pairs={{0,8},{8,16},{16,24},{24,32},{32,40},{40,48},{48,56},{56,64},{64,7... | collective-permute-start | bytes 98312 | tf_op jit(solution)/shard_map/ppermute | solution.py:20
  354.6 6.9 collective-permute-start.7
  356.5 9.0 %collective-permute-start.6 = (f32[64,3,128]{2,1,0:T(4,128)S(1)}, f32[64,3,128]{2,1,0:T(4,128)S(1)}, u32[]{:S(2)}, u32[]{:S(2)}) collective-permute-start(f32[64,3,128]{2,1,0:T(4,128)S(1)} %get-tuple-element.594), channel_id=1, source_target_pairs={{0,8},{8,16},{16,24},{24,32},{32,40},{40,48},{48,56},{56,64},{64,7... | collective-permute-start | bytes 294920 | tf_op jit(solution)/shard_map/ppermute | solution.py:20
  372.3 6.9 collective-permute-start.9
  374.3 9.0 %collective-permute-start.8 = (f32[64,4,128]{2,1,0:T(4,128)S(1)}, f32[64,4,128]{2,1,0:T(4,128)S(1)}, u32[]{:S(2)}, u32[]{:S(2)}) collective-permute-start(f32[64,4,128]{2,1,0:T(4,128)S(1)} %get-tuple-element.596), channel_id=1, source_target_pairs={{0,8},{8,16},{16,24},{24,32},{32,40},{40,48},{48,56},{56,64},{64,7... | collective-permute-start | bytes 393224 | tf_op jit(solution)/shard_map/ppermute | solution.py:20
  458.7 5.9 collective-permute-start.11
  460.7 7.9 %collective-permute-start.10 = (f32[64,1,128]{2,0,1:T(8,128)S(1)}, f32[64,1,128]{2,0,1:T(8,128)S(1)}, u32[]{:S(2)}, u32[]{:S(2)}) collective-permute-start(f32[64,1,128]{2,0,1:T(8,128)S(1)} %get-tuple-element.600), channel_id=1, source_target_pairs={{0,8},{8,16},{16,24},{24,32},{32,40},{40,48},{48,56},{56,64},{64,7... | collective-permute-start | bytes 98312 | tf_op jit(solution)/shard_map/ppermute | solution.py:20
  470.9 5.9 collective-permute-start.13
  472.8 7.9 %collective-permute-start.12 = (f32[64,1,128]{2,0,1:T(8,128)S(1)}, f32[64,1,128]{2,0,1:T(8,128)S(1)}, u32[]{:S(2)}, u32[]{:S(2)}) collective-permute-start(f32[64,1,128]{2,0,1:T(8,128)S(1)} %get-tuple-element.604), channel_id=1, source_target_pairs={{0,8},{8,16},{16,24},{24,32},{32,40},{40,48},{48,56},{56,64},{64,7... | collective-permute-start | bytes 98312 | tf_op jit(solution)/shard_map/ppermute | solution.py:20
  680.0 6.9 collective-permute-start.15
  682.0 22.9 %copy-start.1 = (f32[256,3,128]{2,1,0:T(4,128)S(1)}, f32[256,3,128]{2,1,0:T(4,128)}, u32[]{:S(2)}) copy-start(f32[256,3,128]{2,1,0:T(4,128)} %copy-done) | copy-start | bytes 1179652
  682.0 9.1 %collective-permute-start.14 = (f32[64,3,128]{2,1,0:T(4,128)S(1)}, f32[64,3,128]{2,1,0:T(4,128)S(1)}, u32[]{:S(2)}, u32[]{:S(2)}) collective-permute-start(f32[64,3,128]{2,1,0:T(4,128)S(1)} %get-tuple-element.592), channel_id=1, source_target_pairs={{0,8},{8,16},{16,24},{24,32},{32,40},{40,48},{48,56},{56,64},{64,7... | collective-permute-start | bytes 294920 | tf_op jit(solution)/shard_map/ppermute | solution.py:20
  (23 other events, 74.7 us)
where the time goes:
time: 712 us; the launch traced here: 708 us
  other arithmetic  397 us (56%)
  local copies, waits for them, and re-layouts  159 us (22%)
  starting transfers between devices  67.3 us (9%)
  waiting for transfers between devices  46.5 us (7%)
  blocking collectives  32.8 us (5%)
    reduce_sum x16, other arithmetic, interact(): jnp.sum(coupling * diff_x, axis=2)  184 us
    reduce_sum x16, other arithmetic, interact(): to_self = jnp.sum(kernel * far_mass, axis=2)[:, None, :]  86.9 us
    scatter-add x64, other arithmetic, one_group(): totals = totals.at[target].add(to_other)  81.3 us
    gather x64, local copies, waits for them, and re-layouts, one_group(): partner = combined[target]  38.9 us
    ppermute x8, waiting for transfers between devices, with_halo(): before = lax.ppermute(last, axis, up)  33.7 us
    all_gather x1, blocking collectives, prefix(): gathered = lax.all_gather(part, axis)  32.8 us
    ppermute x8, starting transfers between devices, with_halo(): before = lax.ppermute(last, axis, up)  30.1 us
    gather x32, local copies, waits for them, and re-layouts, one_group(): far_press = None if pressure is None else pressure[target]  27.7 us
  transfers between devices with their start and end apart: 18, of which 12 were waited for; matrix products, arithmetic and copies ran while one was open for 5% of the time, Pallas kernels for 0%

commit v1 on v0

v1 whole, which is shorter than its diff:
```python
import math

import jax
import jax.numpy as jnp
from jax import lax
from jax.experimental import pallas as pl
from jax.experimental.pallas import tpu as pltpu
from jax.sharding import PartitionSpec as P

f32, bf16 = jnp.float32, jnp.bfloat16
SCALE = math.sqrt(math.log2(math.e))


def rounded(x):
    return x.astype(bf16).astype(f32)


def split3(x):
    high = rounded(x)
    rest = x - high
    mid = rounded(rest)
    return high, mid, rest - mid


def split2(x):
    high = x.astype(bf16)
    return high, (x - high.astype(f32)).astype(bf16)


def features(block, centre, row):
    moved = block - centre
    square = jnp.where(row < 3, moved * moved, 0.0)
    half = 0.5 * jnp.sum(square, axis=0, keepdims=True)
    return jnp.where((row == 3) | (row == 4), moved - half, moved)


def left_rows(moved, row):
    h, m, l = split3(moved)
    one = jnp.where(row == 4, 1.0, 0.0)
    a1 = jnp.where(row < 4, h, one)
    a2 = jnp.where(row < 3, h, jnp.where(row == 3, m, one))
    a3 = jnp.where(row < 3, m, jnp.where(row == 3, l, one))
    a4 = jnp.where(row < 3, m, 0.0)
    a5 = jnp.where(row < 3, h, 0.0)
    a6 = jnp.where(row < 3, l, 0.0)
    return jnp.concatenate([a1, a2, a3, a4, a5, a6], 0).astype(bf16)


def right_rows(moved, row):
    h, m, l = split3(moved)
    one = jnp.where(row == 3, 1.0, 0.0)
    low = row < 3
    four = row == 4
    b1 = jnp.where(low | four, h, one)
    b2 = jnp.where(low | four, m, one)
    b3 = jnp.where(low, h, jnp.where(four, l, one))
    b4 = jnp.where(low, m, 0.0)
    b5 = jnp.where(low, l, 0.0)
    b6 = jnp.where(low, h, 0.0)
    return jnp.concatenate([b1, b2, b3, b4, b5, b6], 0).astype(bf16)


def centre_of(block, row):
    return jnp.where(row < 3, jnp.mean(block, axis=1, keepdims=True), 0.0)


def weights_of(own, first, second, row):
    left = left_rows(own, row)
    right = jnp.concatenate(
        [right_rows(own, row), right_rows(first, row), right_rows(second, row)], 1
    )
    exponent = lax.dot_general(
        left, right, (((0,), (0,)), ((), ())), preferred_element_type=f32
    )
    return jnp.exp2(exponent)


def fold(x):
    return jnp.sum(x.reshape(-1, 8, x.shape[-1]), 0)


MOST = 2
STEP = 0.25
UNROLL = 16
GHOSTS = 64


def each(count, body, unroll=8):
    def group(g, _):
        for u in range(unroll):
            body(g * unroll + u)
        return 0

    lax.fori_loop(0, count // unroll, group, 0)


def build_blocks(state, low, high, blocks):
    local = state.shape[0]

    def rows(x, m):
        level = jnp.where(m > 0.0, jnp.log2(jnp.maximum(m, 1e-30)), -300.0)
        return jnp.concatenate([x * SCALE, level, level, jnp.zeros_like(x)], 1)

    def own(g):
        part = state[pl.ds(g * 8, 8)]
        blocks[pl.ds(g * 8, 8)] = rows(part[:, 0:3], part[:, 7:8])

    each(local // 8, own, 4)
    for start, side in ((local, low), (local + GHOSTS, high)):
        def ghost(g, start=start, side=side):
            part = side[pl.ds(g * 8, 8)]
            blocks[pl.ds(start + g * 8, 8)] = rows(part[:, 0:3], part[:, 3:4])

        each(GHOSTS // 8, ghost, 4)


def density_kernel(pairs, state, low, high, local_out, low_out, high_out, blocks, sums):
    local = state.shape[0]
    build_blocks(state, low, high, blocks)
    sums[...] = jnp.zeros_like(sums)
    row = lax.broadcasted_iota(jnp.int32, (8, 128), 0)

    def one(i):
        n1, n2 = pairs[2 * i], pairs[2 * i + 1]
        own = blocks[i]
        centre = centre_of(own, row)
        own, first, second = (
            features(b, centre, row) for b in (own, blocks[n1], blocks[n2])
        )
        m = weights_of(own, first, second, row)
        back = (m[:, 128:256] + m[:, 256:384]).T
        sums[n1] += fold(m[:, 128:256])
        sums[n2] += fold(m[:, 256:384])
        sums[i] += fold(m[:, 0:128]) + fold(back)

    each(local, one, UNROLL)
    for start, count, out in ((0, local, local_out), (local, GHOSTS, low_out), (local + GHOSTS, GHOSTS, high_out)):
        out[...] = jnp.sum(sums[start : start + count], axis=1, keepdims=True)


def pressure_kernel(send, state, own, low, high, density, press, low_pick, high_pick, total):
    total[...] = own[...]

    def back(j):
        total[send[j]] += low[j]

    def back_high(j):
        total[send[GHOSTS + j]] += high[j]

    each(GHOSTS, back)
    each(GHOSTS, back_high)
    rho = total[...] / state[:, 7:8, :]
    density[...] = rho
    press[...] = state[:, 6:7, :] * jnp.exp2(jnp.log2(rho) * (-1.0 / 3.0))

    def pick(j):
        low_pick[j] = press[send[j]]
        high_pick[j] = press[send[GHOSTS + j]]

    each(GHOSTS, pick)


def force_rows(v, y):
    x, qx, q = v[0:3], v[3:6], v[6:7]
    return qx * y[7:8] + x * y[6:7] - q * y[0:3] - y[3:6]


def vector_rows(moved, q):
    x = moved[0:3]
    return jnp.concatenate([x, x * q, q, jnp.ones_like(q)], 0)


def force_kernel(pairs, state, low, high, press_own, press_low, press_high, local_out, low_out, high_out, blocks, press, force):
    local = state.shape[0]
    build_blocks(state, low, high, blocks)
    press[0:local] = press_own[...]
    press[local : local + GHOSTS] = press_low[...]
    press[local + GHOSTS :] = press_high[...]
    force[...] = jnp.zeros_like(force)
    row = lax.broadcasted_iota(jnp.int32, (8, 128), 0)
    zero = jnp.zeros((5, 128), f32)
    dims = (((1,), (1,)), ((), ()))

    def one(i):
        n1, n2 = pairs[2 * i], pairs[2 * i + 1]
        own = blocks[i]
        centre = centre_of(own, row)
        own, first, second = (
            features(b, centre, row) for b in (own, blocks[n1], blocks[n2])
        )
        m = weights_of(own, first, second, row)
        mh, ml = split2(m)
        vs = [vector_rows(b, press[n]) for b, n in ((own, i), (first, n1), (second, n2))]
        vv = [jnp.concatenate(split2(v), 0) for v in vs]
        v_all = jnp.concatenate(vv, 1)
        across = lax.dot_general(
            jnp.concatenate([mh, ml], 1), jnp.concatenate([v_all, v_all], 1), dims,
            preferred_element_type=f32,
        ).T
        across = across[0:8] + across[8:16]
        stacked = jnp.concatenate([mh[:, 128:], ml[:, 128:]], 0)
        down = jnp.dot(
            jnp.concatenate([vv[0], vv[0]], 1), stacked, preferred_element_type=f32
        )
        down = down[0:8] + down[8:16]
        for n, v, y in ((n1, vs[1], down[:, :128]), (n2, vs[2], down[:, 128:]), (i, vs[0], across)):
            force[n] += jnp.concatenate([force_rows(v, y), zero], 0)

    each(local, one, 8)
    for start, count, out in ((0, local, local_out), (local, GHOSTS, low_out), (local + GHOSTS, GHOSTS, high_out)):
        out[...] = force[start : start + count, 0:3, :] * (1.0 / SCALE)


def picks(send, state, low_pick, high_pick):
    def pick(j):
        for side, out in ((0, low_pick), (GHOSTS, high_pick)):
            block = state[send[side + j]]
            out[j] = jnp.concatenate([block[0:3], block[7:8]], 0)

    each(GHOSTS, pick)


def moved_state(send, state, own, low, high, total):
    total[...] = own[...]

    def back(j):
        total[send[j]] += low[j]

    def back_high(j):
        total[send[GHOSTS + j]] += high[j]

    each(GHOSTS, back)
    each(GHOSTS, back_high)
    velocity = state[:, 3:6, :] + STEP * total[...] / state[:, 7:8, :]
    return state[:, 0:3, :] + STEP * velocity, velocity


def move_kernel(send, send_next, state, own, low, high, new, low_pick, high_pick, total):
    position, velocity = moved_state(send, state, own, low, high, total)
    new[:, 0:3, :] = position
    new[:, 3:6, :] = velocity
    new[:, 6:8, :] = state[:, 6:8, :]
    picks(send_next, new, low_pick, high_pick)


def last_kernel(send, state, own, low, high, new, total):
    position, velocity = moved_state(send, state, own, low, high, total)
    new[:, 0:3, :] = position
    new[:, 3:6, :] = velocity


def pack_kernel(index, pos_vel, entropy, masses, packed, outbox):
    packed[:, 0:6, :] = pos_vel[...]
    packed[:, 6:7, :] = entropy[...]
    packed[:, 7:8, :] = masses[...]

    def one(j):
        outbox[j] = packed[index[j]]

    each(outbox.shape[0], one)


def place_kernel(index, send, packed, arrived, state, low_pick, high_pick):
    half = state.shape[0] // 2

    def stay(j):
        state[j] = packed[index[j]]

    def come(j):
        state[half + j] = arrived[index[half + j]]

    each(half, stay)
    each(half, come)
    picks(send, state, low_pick, high_pick)


def call(kernel, name, scalars, operands, outs, scratch=()):
    vmem, smem = (pl.BlockSpec(memory_space=s) for s in (pltpu.VMEM, pltpu.SMEM))
    return pl.pallas_call(
        kernel,
        name=name,
        out_shape=[jax.ShapeDtypeStruct(s, f32) for s in outs],
        in_specs=[smem] * len(scalars) + [vmem] * len(operands),
        out_specs=[vmem] * len(outs),
        scratch_shapes=[pltpu.VMEM(s, f32) for s in scratch],
    )(*scalars, *operands)


def swap(low, high):
    count = lax.axis_size("dom")
    up = [(i, i + 1) for i in range(count - 1)]
    down = [(j, i) for i, j in up]
    return lax.ppermute(high, "dom", up), lax.ppermute(low, "dom", down)


def shards(pos_vel, entropy, masses, destination, ghost_send, pair_list):
    devices = lax.axis_size(("dom", "sub"))
    me = lax.axis_index(("dom", "sub"))
    local = pos_vel.shape[0]
    size = pos_vel.shape[2]
    number = jnp.arange(local, dtype=jnp.int32)
    device = jnp.arange(devices, dtype=jnp.int32)
    slot = jnp.arange(devices * MOST, dtype=jnp.int32)
    same = destination[:, None] == destination[None, :]
    rank = jnp.sum((same & (number[:, None] < number[None, :])).astype(jnp.int32), 0)
    staying = destination == me
    out_slot = jnp.where(staying, -1, destination * MOST + rank)
    pack_index = jnp.sum(jnp.where(out_slot[:, None] == slot[None, :], number[:, None], 0), 0)
    shift = (destination - me) % devices
    wanted = (me - device) % devices
    come = jnp.sum((shift[:, None] == wanted[None, :]).astype(jnp.int32), 0)
    come = jnp.where(device == me, 0, come)
    before = jnp.sum(jnp.where(device[:, None] < device[None, :], come[:, None], 0), 0)
    turn = slot % MOST
    source = slot // MOST
    come_at = source[:, None] == device[None, :]
    first = jnp.sum(jnp.where(come_at, before[None, :], 0), 1)
    many = jnp.sum(jnp.where(come_at, come[None, :], 0), 1)
    place = jnp.where(turn < many, first + turn, -1)
    half = local - devices
    stay_index = jnp.sum(
        jnp.where(staying[:, None] & (rank[:, None] == number[None, :half]), number[:, None], 0), 0
    )
    come_index = jnp.sum(jnp.where(place[:, None] == device[None, :], slot[:, None], 0), 0)
    place_index = jnp.concatenate([stay_index, come_index])

    block = (local, 8, size)
    pick4, pick1, pick3 = ((GHOSTS, r, size) for r in (4, 1, 3))
    one, three = (local, 1, size), (local, 3, size)
    total = local + 2 * GHOSTS
    packed, outbox = call(
        pack_kernel, "pack", (pack_index,), (pos_vel, entropy[:, None], masses[:, None]),
        (block, (devices * MOST, 8, size)),
    )
    arrived = lax.all_to_all(
        outbox.reshape(devices, MOST, 8, size), ("dom", "sub"), split_axis=0, concat_axis=0, tiled=True
    ).reshape(devices * MOST, 8, size)
    state, low_pick, high_pick = call(
        place_kernel, "place", (place_index, ghost_send[0]), (packed, arrived), (block, pick4, pick4)
    )
    steps = ghost_send.shape[0]
    for s in range(steps):
        send, pairs = ghost_send[s], pair_list[s].reshape(-1)
        low, high = swap(low_pick, high_pick)
        own, low_back, high_back = call(
            density_kernel, "density", (pairs,), (state, low, high), (one, pick1, pick1),
            ((total, 8, size), (total, 8, size)),
        )
        low_in, high_in = swap(low_back, high_back)
        density, press, low_pick, high_pick = call(
            pressure_kernel, "pressure", (send,), (state, own, low_in, high_in),
            (one, one, pick1, pick1), (one,),
        )
        press_low, press_high = swap(low_pick, high_pick)
        own, low_back, high_back = call(
            force_kernel, "force", (pairs,), (state, low, high, press, press_low, press_high),
            (three, pick3, pick3), ((total, 8, size), (total, 1, size), (total, 8, size)),
        )
        low_in, high_in = swap(low_back, high_back)
        if s + 1 < steps:
            state, low_pick, high_pick = call(
                move_kernel, "move", (send, ghost_send[s + 1]), (state, own, low_in, high_in),
                (block, pick4, pick4), (three,),
            )
        else:
            (state,) = call(
                last_kernel, "last", (send,), (state, own, low_in, high_in), ((local, 6, size),), (three,)
            )
    return state, density[:, 0]


def solution(mesh):
    both = ("dom", "sub")
    in_specs = (P(both, None, None), P(both, None), P(both, None), P(both), P(None, both), P(None, both, None))
    out_specs = (P(both, None, None), P(both, None))
    return jax.shard_map(shards, mesh=mesh, in_specs=in_specs, out_specs=out_specs, check_vma=False)
```

time: 712 us -> 318 us (0.45)
  other arithmetic: 397 us -> 2.05 us
  Pallas kernels: 0 us -> 191 us
  local copies, waits for them, and re-layouts: 159 us -> 15.2 us
  blocking collectives: 32.8 us -> 0 us
  waiting for transfers between devices: 46.5 us -> 32.2 us
  starting transfers between devices: 67.3 us -> 75.7 us
    reduce_sum x34 -> x6, other arithmetic: 272 us -> 1.41 us  [the longest x1 0.68 us: shards(): jnp.sum(jnp.where(out_slot[:, None] == slot[None, :], number[:, None], 0)...]
    pallas_call x0 -> x10, Pallas kernels: none -> 191 us  [call(): pl.pallas_call(kernel, name=name, out_shape=[jax.ShapeDtypeStruct(s, f32)...]
    scatter-add x68 -> x0, other arithmetic: 103 us -> none  [the longest x64 81.3 us: one_group(): totals = totals.at[target].add(to_other)]
    gather x100 -> x0, local copies, waits for them, and re-layouts: 69.4 us -> none  [the longest x64 38.9 us: one_group(): partner = combined[target]]
    scatter x4 -> x0, local copies, waits for them, and re-layouts: 43 us -> none  [the longest x1 27.1 us: shards(): outbox = jnp.zeros((dev_count * MOST, 8, block_size), jnp.float32).at[out...]
    all_gather x1 -> x0, blocking collectives: 32.8 us -> none  [prefix(): gathered = lax.all_gather(part, axis)]
    ppermute x16, waiting for transfers between devices: 36 us -> 17 us  [swap(): return (lax.ppermute(high, 'dom', up), lax.ppermute(low, 'dom', down))]
    ppermute x16, starting transfers between devices: 47.1 us -> 65.3 us  [swap(): return (lax.ppermute(high, 'dom', up), lax.ppermute(low, 'dom', down))]
  transfers between devices with their start and end apart: 18 -> 17, of which waited for: 12 -> 17; matrix products, arithmetic and copies ran while one was open for 5% -> 1% of each run, Pallas kernels for 0% -> 0%
where the time goes in v1:
time: 318 us; the launch traced here: 317 us
  Pallas kernels  191 us (60%)
  starting transfers between devices  75.7 us (24%)
  waiting for transfers between devices  32.2 us (10%)
  local copies, waits for them, and re-layouts  15.2 us (5%)
    pallas_call x10, Pallas kernels, call(): pl.pallas_call(kernel, name=name, out_shape=[jax.ShapeDtypeStruct(s, f32)...  191 us
    ppermute x16, starting transfers between devices, swap(): return (lax.ppermute(high, 'dom', up), lax.ppermute(low, 'dom', down))  65.3 us
    ppermute x16, waiting for transfers between devices, swap(): return (lax.ppermute(high, 'dom', up), lax.ppermute(low, 'dom', down))  17 us
    all_to_all x1, waiting for transfers between devices, shards(): lax.all_to_all(outbox.reshape(devices, MOST, 8, size), ('dom', 'sub'), sp...  15.1 us
    unnamed x44, local copies, waits for them, and re-layouts  12.2 us
    all_to_all x1, starting transfers between devices, shards(): lax.all_to_all(outbox.reshape(devices, MOST, 8, size), ('dom', 'sub'), sp...  10.4 us
  transfers between devices with their start and end apart: 17, of which 17 were waited for; matrix products, arithmetic and copies ran while one was open for 1% of the time, Pallas kernels for 0%

profile of v1, /device:TPU:8, one launch (start us, length us, event | category | flops | bytes accessed | tf_op | source)
XLA Modules:
  0.0 316.9 jit_solution(1977053454616663397)
XLA Ops:
  4.7 3.4 %pack.1 = (f32[256,8,128]{2,1,0:T(8,128)}, f32[256,8,128]{2,1,0:T(8,128)}) custom-call(s32[256]{0:T(256)} %select_reduce_fusion.index, f32[256,6,128]{2,1,0:T(8,128)} %copy.14.pos_vel, f32[256,1,128]{2,1,0:T(1,128)} %bitcast.11, f32[256,1,128]{2,1,0:T(1,128)} %bitcast.12), custom_call_target="tpu_custom_call" | custom-call | tf_op jit(solution)/shard_map/pack/pallas_call | solution.py:279
  8.1 10.4 %all-to-all-start = ((f32[128,2,8,128]{3,2,1,0:T(8,128)}), f32[128,2,8,128]{3,2,1,0:T(8,128)S(1)}, u32[]{:S(2)}, u32[]{:S(2)}) async-start(f32[128,2,8,128]{3,2,1,0:T(8,128)} %bitcast.10), calls=%async_computation | async-start | bytes 2097152 | tf_op jit(solution)/shard_map/all_to_all | solution.py:335
  21.7 15.1 %all-to-all-done = f32[128,2,8,128]{3,2,1,0:T(8,128)S(1)} async-done(((f32[128,2,8,128]{3,2,1,0:T(8,128)}), f32[128,2,8,128]{3,2,1,0:T(8,128)S(1)}, u32[]{:S(2)}, u32[]{:S(2)}) %all-to-all-start) | async-done | bytes 1048608 | tf_op jit(solution)/shard_map/all_to_all | solution.py:335
  37.9 3.2 %place.1 = (f32[256,8,128]{2,1,0:T(8,128)}, f32[64,4,128]{2,1,0:T(4,128)}, f32[64,4,128]{2,1,0:T(4,128)}) custom-call(s32[256]{0:T(256)} %pad_add_fusion.index, s32[128]{0:T(128)} %get-tuple-element.68.send, f32[256,8,128]{2,1,0:T(8,128)} %get-tuple-element.29.packed, f32[256,8,128]{2,1,0:T(8,128)} %bitcast.9), custom_call_target="tpu_custom_call" | custom-call | tf_op jit(solution)/shard_map/place/pallas_call | solution.py:279
  43.8 5.3 %collective-permute-start.1 = (f32[64,4,128]{2,1,0:T(4,128)}, f32[64,4,128]{2,1,0:T(4,128)S(1)}, u32[]{:S(2)}, u32[]{:S(2)}) collective-permute-start(f32[64,4,128]{2,1,0:T(4,128)} %get-tuple-element.33), channel_id=1, source_target_pairs={{8,0},{16,8},{24,16},{32,24},{40,32},{48,40},{56,48},{64,56},{72,6... | collective-permute-start | bytes 393224 | tf_op jit(solution)/shard_map/ppermute | solution.py:293
  52.5 20.1 %density.2 = (f32[256,1,128]{2,1,0:T(1,128)}, f32[64,1,128]{2,1,0:T(1,128)}, f32[64,1,128]{2,1,0:T(1,128)}) custom-call(s32[512]{0:T(512)} %reshape_squeeze.6.pairs, f32[256,8,128]{2,1,0:T(8,128)} %get-tuple-element.31.state, f32[64,4,128]{2,1,0:T(4,128)} %copy-done.1, f32[64,4,128]{2,1,0:T(4,128)} %copy-done.2), custom_call_target="tpu_custom_call" | custom-call | tf_op jit(solution)/shard_map/density/pallas_call | solution.py:279
  74.6 6.3 %collective-permute-start.3 = (f32[64,1,128]{2,1,0:T(1,128)}, f32[64,1,128]{2,1,0:T(1,128)S(1)}, u32[]{:S(2)}, u32[]{:S(2)}) collective-permute-start(f32[64,1,128]{2,1,0:T(1,128)} %get-tuple-element.36), channel_id=1, source_target_pairs={{8,0},{16,8},{24,16},{32,24},{40,32},{48,40},{56,48},{64,56},{72,6... | collective-permute-start | bytes 98312 | tf_op jit(solution)/shard_map/ppermute | solution.py:293
  83.4 3.1 pressure.2
  86.5 2.7 collective-permute-start.4
  89.2 5.5 %collective-permute-start.5 = (f32[64,1,128]{2,1,0:T(1,128)}, f32[64,1,128]{2,1,0:T(1,128)S(1)}, u32[]{:S(2)}, u32[]{:S(2)}) collective-permute-start(f32[64,1,128]{2,1,0:T(1,128)} %get-tuple-element.39), channel_id=1, source_target_pairs={{8,0},{16,8},{24,16},{32,24},{40,32},{48,40},{56,48},{64,56},{72,6... | collective-permute-start | bytes 98312 | tf_op jit(solution)/shard_map/ppermute | solution.py:293
  97.1 65.5 %force.2 = (f32[256,3,128]{2,1,0:T(4,128)}, f32[64,3,128]{2,1,0:T(4,128)}, f32[64,3,128]{2,1,0:T(4,128)}) custom-call(s32[512]{0:T(512)} %reshape_squeeze.6.pairs, f32[256,8,128]{2,1,0:T(8,128)} %get-tuple-element.31.state, f32[64,4,128]{2,1,0:T(4,128)} %copy-done.1, f32[64,4,128]{2,1,0:T(4,128)} %copy-done.2, f32[256,1,128]{2,1,0:T(1,128)} %get-tuple-element.37.press_own, ...), custom_call_target="tpu_custom_call" | custom-call | tf_op jit(solution)/shard_map/force/pallas_call | solution.py:279
  162.7 2.7 collective-permute-start.6
  165.4 5.5 %collective-permute-start.7 = (f32[64,3,128]{2,1,0:T(4,128)}, f32[64,3,128]{2,1,0:T(4,128)S(1)}, u32[]{:S(2)}, u32[]{:S(2)}) collective-permute-start(f32[64,3,128]{2,1,0:T(4,128)} %get-tuple-element.42), channel_id=1, source_target_pairs={{8,0},{16,8},{24,16},{32,24},{40,32},{48,40},{56,48},{64,56},{72,6... | collective-permute-start | bytes 294920 | tf_op jit(solution)/shard_map/ppermute | solution.py:293
  174.3 3.6 %move.1 = (f32[256,8,128]{2,1,0:T(8,128)}, f32[64,4,128]{2,1,0:T(4,128)}, f32[64,4,128]{2,1,0:T(4,128)}) custom-call(s32[128]{0:T(128)} %get-tuple-element.68.send, s32[128]{0:T(128)} %get-tuple-element.69.send_next.send, f32[256,8,128]{2,1,0:T(8,128)} %get-tuple-element.31.state, f32[256,3,128]{2,1,0:T(4,128)} %get-tuple-element.40.own, ...), custom_call_target="tpu_custom_call" | custom-call | tf_op jit(solution)/shard_map/move/pallas_call | solution.py:279
  177.9 2.8 collective-permute-start.8
  180.7 5.5 %collective-permute-start.9 = (f32[64,4,128]{2,1,0:T(4,128)}, f32[64,4,128]{2,1,0:T(4,128)S(1)}, u32[]{:S(2)}, u32[]{:S(2)}) collective-permute-start(f32[64,4,128]{2,1,0:T(4,128)} %get-tuple-element.45), channel_id=1, source_target_pairs={{8,0},{16,8},{24,16},{32,24},{40,32},{48,40},{56,48},{64,56},{72,6... | collective-permute-start | bytes 393224 | tf_op jit(solution)/shard_map/ppermute | solution.py:293
  189.6 20.1 %density.3 = (f32[256,1,128]{2,1,0:T(1,128)}, f32[64,1,128]{2,1,0:T(1,128)}, f32[64,1,128]{2,1,0:T(1,128)}) custom-call(s32[512]{0:T(512)} %reshape_squeeze.7.pairs, f32[256,8,128]{2,1,0:T(8,128)} %get-tuple-element.43.state, f32[64,4,128]{2,1,0:T(4,128)} %copy-done.3, f32[64,4,128]{2,1,0:T(4,128)} %copy-done.4), custom_call_target="tpu_custom_call" | custom-call | tf_op jit(solution)/shard_map/density/pallas_call | solution.py:279
  209.7 2.8 collective-permute-start.10
  212.6 5.5 %collective-permute-start.11 = (f32[64,1,128]{2,1,0:T(1,128)}, f32[64,1,128]{2,1,0:T(1,128)S(1)}, u32[]{:S(2)}, u32[]{:S(2)}) collective-permute-start(f32[64,1,128]{2,1,0:T(1,128)} %get-tuple-element.48), channel_id=1, source_target_pairs={{8,0},{16,8},{24,16},{32,24},{40,32},{48,40},{56,48},{64,56},{72,6... | collective-permute-start | bytes 98312 | tf_op jit(solution)/shard_map/ppermute | solution.py:293
  220.5 3.0 pressure.3
  226.2 5.5 %collective-permute-start.13 = (f32[64,1,128]{2,1,0:T(1,128)}, f32[64,1,128]{2,1,0:T(1,128)S(1)}, u32[]{:S(2)}, u32[]{:S(2)}) collective-permute-start(f32[64,1,128]{2,1,0:T(1,128)} %get-tuple-element.51), channel_id=1, source_target_pairs={{8,0},{16,8},{24,16},{32,24},{40,32},{48,40},{56,48},{64,56},{72,6... | collective-permute-start | bytes 98312 | tf_op jit(solution)/shard_map/ppermute | solution.py:293
  234.2 65.5 %force.3 = (f32[256,3,128]{2,1,0:T(4,128)}, f32[64,3,128]{2,1,0:T(4,128)}, f32[64,3,128]{2,1,0:T(4,128)}) custom-call(s32[512]{0:T(512)} %reshape_squeeze.7.pairs, f32[256,8,128]{2,1,0:T(8,128)} %get-tuple-element.43.state, f32[64,4,128]{2,1,0:T(4,128)} %copy-done.3, f32[64,4,128]{2,1,0:T(4,128)} %copy-done.4, f32[256,1,128]{2,1,0:T(1,128)} %get-tuple-element.49.press_own, ...), custom_call_target="tpu_custom_call" | custom-call | tf_op jit(solution)/shard_map/force/pallas_call | solution.py:279
  302.4 5.5 %collective-permute-start.15 = (f32[64,3,128]{2,1,0:T(4,128)}, f32[64,3,128]{2,1,0:T(4,128)S(1)}, u32[]{:S(2)}, u32[]{:S(2)}) collective-permute-start(f32[64,3,128]{2,1,0:T(4,128)} %get-tuple-element.54), channel_id=1, source_target_pairs={{8,0},{16,8},{24,16},{32,24},{40,32},{48,40},{56,48},{64,56},{72,6... | collective-permute-start | bytes 294920 | tf_op jit(solution)/shard_map/ppermute | solution.py:293
  311.4 3.2 %last.1 = f32[256,6,128]{2,1,0:T(8,128)} custom-call(s32[128]{0:T(128)} %get-tuple-element.69.send_next.send, f32[256,8,128]{2,1,0:T(8,128)} %get-tuple-element.43.state, f32[256,3,128]{2,1,0:T(4,128)} %get-tuple-element.52.own, f32[64,3,128]{2,1,0:T(4,128)} %copy-done.7, f32[64,3,128]{2,1,0:T(4,128)} %copy-done.8), custom_call_target="tpu_custom_call" | custom-call | tf_op jit(solution)/shard_map/last/pallas_call | solution.py:279
  (86 shorter events, 44.2 us)
Async XLA Ops:
  8.1 28.8 %all-to-all-start = ((f32[128,2,8,128]{3,2,1,0:T(8,128)}), f32[128,2,8,128]{3,2,1,0:T(8,128)S(1)}, u32[]{:S(2)}, u32[]{:S(2)}) async-start(f32[128,2,8,128]{3,2,1,0:T(8,128)} %bitcast.10), calls=%async_computation | async-start | bytes 2097152 | tf_op jit(solution)/shard_map/all_to_all | solution.py:335
  37.9 11.2 %copy-start.18 = (s32[2,256,2]{1,2,0:T(2,128)S(1)}, s32[2,256,2]{1,2,0:T(2,128)}, u32[]{:S(2)}) copy-start(s32[2,256,2]{1,2,0:T(2,128)} %param.11) | copy-start | bytes 12292
  41.1 9.2 %collective-permute-start = (f32[64,4,128]{2,1,0:T(4,128)}, f32[64,4,128]{2,1,0:T(4,128)S(1)}, u32[]{:S(2)}, u32[]{:S(2)}) collective-permute-start(f32[64,4,128]{2,1,0:T(4,128)} %get-tuple-element.32), channel_id=1, source_target_pairs={{0,8},{8,16},{16,24},{24,32},{32,40},{40,48},{48,56},{56,64},{64,7... | collective-permute-start | bytes 393224 | tf_op jit(solution)/shard_map/ppermute | solution.py:293
  43.8 8.1 %collective-permute-start.1 = (f32[64,4,128]{2,1,0:T(4,128)}, f32[64,4,128]{2,1,0:T(4,128)S(1)}, u32[]{:S(2)}, u32[]{:S(2)}) collective-permute-start(f32[64,4,128]{2,1,0:T(4,128)} %get-tuple-element.33), channel_id=1, source_target_pairs={{8,0},{16,8},{24,16},{32,24},{40,32},{48,40},{56,48},{64,56},{72,6... | collective-permute-start | bytes 393224 | tf_op jit(solution)/shard_map/ppermute | solution.py:293
  50.3 1.6 copy-start.1
  72.7 8.4 %collective-permute-start.2 = (f32[64,1,128]{2,1,0:T(1,128)}, f32[64,1,128]{2,1,0:T(1,128)S(1)}, u32[]{:S(2)}, u32[]{:S(2)}) collective-permute-start(f32[64,1,128]{2,1,0:T(1,128)} %get-tuple-element.35), channel_id=1, source_target_pairs={{0,8},{8,16},{16,24},{24,32},{32,40},{40,48},{48,56},{56,64},{64,7... | collective-permute-start | bytes 98312 | tf_op jit(solution)/shard_map/ppermute | solution.py:293
  74.6 8.2 %collective-permute-start.3 = (f32[64,1,128]{2,1,0:T(1,128)}, f32[64,1,128]{2,1,0:T(1,128)S(1)}, u32[]{:S(2)}, u32[]{:S(2)}) collective-permute-start(f32[64,1,128]{2,1,0:T(1,128)} %get-tuple-element.36), channel_id=1, source_target_pairs={{8,0},{16,8},{24,16},{32,24},{40,32},{48,40},{56,48},{64,56},{72,6... | collective-permute-start | bytes 98312 | tf_op jit(solution)/shard_map/ppermute | solution.py:293
  81.1 1.7 copy-start.11
  86.5 8.3 %collective-permute-start.4 = (f32[64,1,128]{2,1,0:T(1,128)}, f32[64,1,128]{2,1,0:T(1,128)S(1)}, u32[]{:S(2)}, u32[]{:S(2)}) collective-permute-start(f32[64,1,128]{2,1,0:T(1,128)} %get-tuple-element.38), channel_id=1, source_target_pairs={{0,8},{8,16},{16,24},{24,32},{32,40},{40,48},{48,56},{56,64},{64,7... | collective-permute-start | bytes 98312 | tf_op jit(solution)/shard_map/ppermute | solution.py:293
  89.2 7.4 %collective-permute-start.5 = (f32[64,1,128]{2,1,0:T(1,128)}, f32[64,1,128]{2,1,0:T(1,128)S(1)}, u32[]{:S(2)}, u32[]{:S(2)}) collective-permute-start(f32[64,1,128]{2,1,0:T(1,128)} %get-tuple-element.39), channel_id=1, source_target_pairs={{8,0},{16,8},{24,16},{32,24},{40,32},{48,40},{56,48},{64,56},{72,6... | collective-permute-start | bytes 98312 | tf_op jit(solution)/shard_map/ppermute | solution.py:293
  94.8 1.7 copy-start.9
  162.7 9.4 %collective-permute-start.6 = (f32[64,3,128]{2,1,0:T(4,128)}, f32[64,3,128]{2,1,0:T(4,128)S(1)}, u32[]{:S(2)}, u32[]{:S(2)}) collective-permute-start(f32[64,3,128]{2,1,0:T(4,128)} %get-tuple-element.41), channel_id=1, source_target_pairs={{0,8},{8,16},{16,24},{24,32},{32,40},{40,48},{48,56},{56,64},{64,7... | collective-permute-start | bytes 294920 | tf_op jit(solution)/shard_map/ppermute | solution.py:293
  165.4 8.3 %collective-permute-start.7 = (f32[64,3,128]{2,1,0:T(4,128)}, f32[64,3,128]{2,1,0:T(4,128)S(1)}, u32[]{:S(2)}, u32[]{:S(2)}) collective-permute-start(f32[64,3,128]{2,1,0:T(4,128)} %get-tuple-element.42), channel_id=1, source_target_pairs={{8,0},{16,8},{24,16},{32,24},{40,32},{48,40},{56,48},{64,56},{72,6... | collective-permute-start | bytes 294920 | tf_op jit(solution)/shard_map/ppermute | solution.py:293
  177.9 9.5 %collective-permute-start.8 = (f32[64,4,128]{2,1,0:T(4,128)}, f32[64,4,128]{2,1,0:T(4,128)S(1)}, u32[]{:S(2)}, u32[]{:S(2)}) collective-permute-start(f32[64,4,128]{2,1,0:T(4,128)} %get-tuple-element.44), channel_id=1, source_target_pairs={{0,8},{8,16},{16,24},{24,32},{32,40},{40,48},{48,56},{56,64},{64,7... | collective-permute-start | bytes 393224 | tf_op jit(solution)/shard_map/ppermute | solution.py:293
  180.7 8.3 %collective-permute-start.9 = (f32[64,4,128]{2,1,0:T(4,128)}, f32[64,4,128]{2,1,0:T(4,128)S(1)}, u32[]{:S(2)}, u32[]{:S(2)}) collective-permute-start(f32[64,4,128]{2,1,0:T(4,128)} %get-tuple-element.45), channel_id=1, source_target_pairs={{8,0},{16,8},{24,16},{32,24},{40,32},{48,40},{56,48},{64,56},{72,6... | collective-permute-start | bytes 393224 | tf_op jit(solution)/shard_map/ppermute | solution.py:293
  209.7 8.4 %collective-permute-start.10 = (f32[64,1,128]{2,1,0:T(1,128)}, f32[64,1,128]{2,1,0:T(1,128)S(1)}, u32[]{:S(2)}, u32[]{:S(2)}) collective-permute-start(f32[64,1,128]{2,1,0:T(1,128)} %get-tuple-element.47), channel_id=1, source_target_pairs={{0,8},{8,16},{16,24},{24,32},{32,40},{40,48},{48,56},{56,64},{64,7... | collective-permute-start | bytes 98312 | tf_op jit(solution)/shard_map/ppermute | solution.py:293
  212.6 7.4 %collective-permute-start.11 = (f32[64,1,128]{2,1,0:T(1,128)}, f32[64,1,128]{2,1,0:T(1,128)S(1)}, u32[]{:S(2)}, u32[]{:S(2)}) collective-permute-start(f32[64,1,128]{2,1,0:T(1,128)} %get-tuple-element.48), channel_id=1, source_target_pairs={{8,0},{16,8},{24,16},{32,24},{40,32},{48,40},{56,48},{64,56},{72,6... | collective-permute-start | bytes 98312 | tf_op jit(solution)/shard_map/ppermute | solution.py:293
  218.2 1.7 copy-start.12
  223.6 8.3 %collective-permute-start.12 = (f32[64,1,128]{2,1,0:T(1,128)}, f32[64,1,128]{2,1,0:T(1,128)S(1)}, u32[]{:S(2)}, u32[]{:S(2)}) collective-permute-start(f32[64,1,128]{2,1,0:T(1,128)} %get-tuple-element.50), channel_id=1, source_target_pairs={{0,8},{8,16},{16,24},{24,32},{32,40},{40,48},{48,56},{56,64},{64,7... | collective-permute-start | bytes 98312 | tf_op jit(solution)/shard_map/ppermute | solution.py:293
  226.2 7.4 %collective-permute-start.13 = (f32[64,1,128]{2,1,0:T(1,128)}, f32[64,1,128]{2,1,0:T(1,128)S(1)}, u32[]{:S(2)}, u32[]{:S(2)}) collective-permute-start(f32[64,1,128]{2,1,0:T(1,128)} %get-tuple-element.51), channel_id=1, source_target_pairs={{8,0},{16,8},{24,16},{32,24},{40,32},{48,40},{56,48},{64,56},{72,6... | collective-permute-start | bytes 98312 | tf_op jit(solution)/shard_map/ppermute | solution.py:293
  231.9 1.7 copy-start.10
  299.7 9.4 %collective-permute-start.14 = (f32[64,3,128]{2,1,0:T(4,128)}, f32[64,3,128]{2,1,0:T(4,128)S(1)}, u32[]{:S(2)}, u32[]{:S(2)}) collective-permute-start(f32[64,3,128]{2,1,0:T(4,128)} %get-tuple-element.53), channel_id=1, source_target_pairs={{0,8},{8,16},{16,24},{24,32},{32,40},{40,48},{48,56},{56,64},{64,7... | collective-permute-start | bytes 294920 | tf_op jit(solution)/shard_map/ppermute | solution.py:293
  302.4 8.3 %collective-permute-start.15 = (f32[64,3,128]{2,1,0:T(4,128)}, f32[64,3,128]{2,1,0:T(4,128)S(1)}, u32[]{:S(2)}, u32[]{:S(2)}) collective-permute-start(f32[64,3,128]{2,1,0:T(4,128)} %get-tuple-element.54), channel_id=1, source_target_pairs={{8,0},{16,8},{24,16},{32,24},{40,32},{48,40},{56,48},{64,56},{72,6... | collective-permute-start | bytes 294920 | tf_op jit(solution)/shard_map/ppermute | solution.py:293
  309.1 1.6 copy-start.7
  (15 other events, 11.8 us)

commit v2 on v1

v2 whole, which is shorter than its diff:
```python
import functools
import math

import jax
import jax.numpy as jnp
from jax import lax
from jax.experimental import pallas as pl
from jax.experimental.pallas import tpu as pltpu
from jax.sharding import PartitionSpec as P

f32, bf16 = jnp.float32, jnp.bfloat16
SCALE = math.sqrt(math.log2(math.e))


def rounded(x):
    return x.astype(bf16).astype(f32)


def split3(x):
    high = rounded(x)
    rest = x - high
    mid = rounded(rest)
    return high, mid, rest - mid


def split2(x):
    high = x.astype(bf16)
    return high, (x - high.astype(f32)).astype(bf16)


def features(block, centre, row):
    moved = block - centre
    square = jnp.where(row < 3, moved * moved, 0.0)
    half = 0.5 * jnp.sum(square, axis=0, keepdims=True)
    return jnp.where((row == 3) | (row == 4), moved - half, moved)


def left_rows(moved, row):
    h, m, l = split3(moved)
    one = jnp.where(row == 4, 1.0, 0.0)
    a1 = jnp.where(row < 4, h, one)
    a2 = jnp.where(row < 3, h, jnp.where(row == 3, m, one))
    a3 = jnp.where(row < 3, m, jnp.where(row == 3, l, one))
    a4 = jnp.where(row < 3, m, 0.0)
    a5 = jnp.where(row < 3, h, 0.0)
    a6 = jnp.where(row < 3, l, 0.0)
    return jnp.concatenate([a1, a2, a3, a4, a5, a6], 0).astype(bf16)


def right_rows(moved, row):
    h, m, l = split3(moved)
    one = jnp.where(row == 3, 1.0, 0.0)
    low = row < 3
    four = row == 4
    b1 = jnp.where(low | four, h, one)
    b2 = jnp.where(low | four, m, one)
    b3 = jnp.where(low, h, jnp.where(four, l, one))
    b4 = jnp.where(low, m, 0.0)
    b5 = jnp.where(low, l, 0.0)
    b6 = jnp.where(low, h, 0.0)
    return jnp.concatenate([b1, b2, b3, b4, b5, b6], 0).astype(bf16)


def centre_of(block, row):
    return jnp.where(row < 3, jnp.mean(block, axis=1, keepdims=True), 0.0)


def weights_of(left, parts, row):
    right = jnp.concatenate([right_rows(p, row) for p in parts], 1)
    exponent = lax.dot_general(
        left_rows(left, row), right, (((0,), (0,)), ((), ())), preferred_element_type=f32
    )
    return jnp.exp2(exponent)


def fold(x):
    return jnp.sum(x.reshape(-1, 8, x.shape[-1]), 0)


MOST = 2
STEP = 0.25
UNROLL = 8
GHOSTS = 64
NONE = -300.0


def each(count, body, unroll=8):
    def group(g, _):
        for u in range(unroll):
            body(g * unroll + u)
        return 0

    lax.fori_loop(0, count // unroll, group, 0)


def column_sum(x):
    return jnp.sum(fold(x), axis=0, keepdims=True)


def force_rows(v, y):
    x, qx, q = v[0:3], v[3:6], v[6:7]
    return qx * y[7:8] + x * y[6:7] - q * y[0:3] - y[3:6]


def vector_rows(moved, q):
    x = moved[0:3]
    return jnp.concatenate([x, x * q, q, jnp.ones_like(q)], 0)


def halves(v):
    return jnp.concatenate(split2(v), 0)


def join(y):
    return y[0:8] + y[8:16]


def lanes(rows):
    return jnp.concatenate([rows[c : c + 1] for c in range(3)], 1)


def routed_sum(chosen, first, rows, values):
    number = lax.broadcasted_iota(jnp.int32, (rows, chosen.shape[1]), 0) + first
    hot = jnp.where(number == chosen, 1.0, 0.0).astype(bf16)
    width = values.shape[1]
    parts = jnp.concatenate(split3(values), 1).astype(bf16)
    out = jnp.dot(hot, parts, preferred_element_type=f32)
    return out[:, :width] + out[:, width : 2 * width] + out[:, 2 * width :]


def step_kernel(
    domains, steps, send, pairs, send_row, pair_row, start, final, density,
    state, blocks, press, entropy, masses, own_m, pair_m, r_own, r_pair, f_own, f_pair, f_sum,
    p_out, p_in, r_out, r_in, q_out, q_in, f_out, f_in, send_sem, recv_sem,
):
    local = start.shape[0]
    total = local + 2 * GHOSTS
    dom = lax.axis_index("dom")
    has_low, has_high = dom > 0, dom < domains - 1
    row = lax.broadcasted_iota(jnp.int32, (8, 128), 0)

    def links(s, phase, out, into):
        def copy(side, target):
            return pltpu.make_async_remote_copy(
                src_ref=out.at[s, side],
                dst_ref=into.at[s, 1 - side],
                send_sem=send_sem.at[s, phase, side],
                recv_sem=recv_sem.at[s, phase, 1 - side],
                device_id={"dom": target},
                device_id_type=pl.DeviceIdType.MESH,
            )

        return copy(0, dom - 1), copy(1, dom + 1)

    def begin(s, phase, out, into):
        to_low, to_high = links(s, phase, out, into)
        pl.when(has_low)(to_low.start)
        pl.when(has_high)(to_high.start)

    def finish(s, phase, out, into):
        to_low, to_high = links(s, phase, out, into)

        @pl.when(has_low)
        def _():
            to_low.wait_send()
            to_high.wait_recv()

        @pl.when(has_high)
        def _():
            to_high.wait_send()
            to_low.wait_recv()

    if domains > 1:
        barrier = pltpu.get_barrier_semaphore()

        def greet(target):
            pl.semaphore_signal(
                barrier, inc=1, device_id={"dom": target}, device_id_type=pl.DeviceIdType.MESH
            )

        pl.when(has_low)(lambda: greet(dom - 1))
        pl.when(has_high)(lambda: greet(dom + 1))

    for side, has in ((0, has_low), (1, has_high)):

        @pl.when(jnp.logical_not(has))
        def _(side=side):
            for s in range(steps):
                p_in[s, side] = jnp.concatenate(
                    [jnp.zeros((GHOSTS, 3, 128), f32), jnp.full((GHOSTS, 1, 128), NONE, f32)], 1
                )
                for into in (r_in, q_in, f_in):
                    into[s, side] = jnp.zeros(into.shape[2:], f32)

    def enter(i):
        block = start[i]
        state[i] = block
        entropy[pl.ds(i, 1), :] = block[6:7]
        masses[pl.ds(i, 1), :] = block[7:8]

    each(local, enter)

    for s in range(steps):

        def scaled(i):
            block = state[i]
            level = jnp.log2(block[7:8])
            blocks[i] = jnp.concatenate(
                [block[0:3] * SCALE, level, level, jnp.zeros((3, 128), f32)], 0
            )

        each(local, scaled)

        def pick(j):
            for side in range(2):
                p_out[s, side, j] = blocks[send[s, side * GHOSTS + j]][0:4]

        each(GHOSTS, pick)
        if s == 0 and domains > 1:
            pl.semaphore_wait(barrier, has_low.astype(jnp.int32) + has_high.astype(jnp.int32))
        if domains > 1:
            begin(s, 0, p_out, p_in)

        def own_density(i):
            block = blocks[i]
            block = features(block, centre_of(block, row), row)
            m = weights_of(block, (block,), row)
            r_own[pl.ds(i, 1), :] = column_sum(m)
            h, l = split2(m)
            own_m[i, 0:128] = h
            own_m[i, 128:256] = l

        each(local, own_density, UNROLL)
        if domains > 1:
            finish(s, 0, p_out, p_in)

        def ghost(j):
            for side in range(2):
                block = p_in[s, side, j]
                blocks[local + side * GHOSTS + j] = jnp.concatenate(
                    [block, block[3:4], jnp.zeros((3, 128), f32)], 0
                )

        each(GHOSTS, ghost)

        def pair_density(i):
            block = blocks[i]
            centre = centre_of(block, row)
            own, first, second = (
                features(b, centre, row)
                for b in (block, blocks[pairs[s, 2 * i]], blocks[pairs[s, 2 * i + 1]])
            )
            m = weights_of(own, (first, second), row)
            sums = column_sum(m)
            r_pair[pl.ds(2 * i, 1), :] = sums[:, :128]
            r_pair[pl.ds(2 * i + 1, 1), :] = sums[:, 128:]
            r_own[pl.ds(i, 1), :] += column_sum((m[:, :128] + m[:, 128:]).T)
            h, l = split2(m)
            pair_m[i, :, 0:256] = h
            pair_m[i, :, 256:512] = l

        each(local, pair_density, UNROLL)
        chosen = pair_row[s]
        sent = send_row[s]
        for side in range(2):
            r_out[s, side] = routed_sum(chosen, local + side * GHOSTS, GHOSTS, r_pair[...])
        for part in range(0, local, 128):
            r_own[part : part + 128] += routed_sum(chosen, part, 128, r_pair[...])
        if domains > 1:
            begin(s, 1, r_out, r_in)
            finish(s, 1, r_out, r_in)
        incoming = jnp.concatenate([r_in[s, 0], r_in[s, 1]], 0)
        rho = (r_own[...] + routed_sum(sent, 0, local, incoming)) / masses[...]
        if s == steps - 1:
            density[...] = rho
        press[0:local] = entropy[...] * jnp.exp2(jnp.log2(rho) * (-1.0 / 3.0))

        def pick_press(j):
            for side in range(2):
                q_out[s, side, pl.ds(j, 1), :] = press[pl.ds(send[s, side * GHOSTS + j], 1), :]

        each(GHOSTS, pick_press)
        if domains > 1:
            begin(s, 2, q_out, q_in)

        def own_force(i):
            block = blocks[i]
            v = vector_rows(block - centre_of(block, row), press[pl.ds(i, 1), :])
            vv = halves(v)
            y = join(
                jnp.dot(jnp.concatenate([vv, vv], 1), own_m[i], preferred_element_type=f32)
            )
            f_own[pl.ds(i, 1), :] = lanes(force_rows(v, y))

        each(local, own_force, UNROLL)
        if domains > 1:
            finish(s, 2, q_out, q_in)
        press[local : local + GHOSTS] = q_in[s, 0]
        press[local + GHOSTS : total] = q_in[s, 1]

        def pair_force(i):
            block = blocks[i]
            centre = centre_of(block, row)
            n1, n2 = pairs[s, 2 * i], pairs[s, 2 * i + 1]
            vs = [
                vector_rows(b - centre, press[pl.ds(n, 1), :])
                for b, n in ((block, i), (blocks[n1], n1), (blocks[n2], n2))
            ]
            own, first, second = (halves(v) for v in vs)
            far = jnp.concatenate([first, second, first, second], 1)
            across = lax.dot_general(
                pair_m[i], far, (((1,), (1,)), ((), ())), preferred_element_type=f32
            ).T
            f_own[pl.ds(i, 1), :] += lanes(force_rows(vs[0], join(across)))
            stacked = jnp.concatenate([pair_m[i, :, 0:256], pair_m[i, :, 256:512]], 0)
            down = join(
                jnp.dot(jnp.concatenate([own, own], 1), stacked, preferred_element_type=f32)
            )
            f_pair[pl.ds(2 * i, 1), :] = lanes(force_rows(vs[1], down[:, :128]))
            f_pair[pl.ds(2 * i + 1, 1), :] = lanes(force_rows(vs[2], down[:, 128:]))

        each(local, pair_force, UNROLL)
        for side in range(2):
            f_out[s, side] = routed_sum(chosen, local + side * GHOSTS, GHOSTS, f_pair[...])
        for part in range(0, local, 128):
            f_own[part : part + 128] += routed_sum(chosen, part, 128, f_pair[...])
        if domains > 1:
            begin(s, 3, f_out, f_in)
            finish(s, 3, f_out, f_in)
        incoming = jnp.concatenate([f_in[s, 0], f_in[s, 1]], 0)
        for part in range(0, local, 128):
            f_sum[part : part + 128] = f_own[part : part + 128] + routed_sum(sent, part, 128, incoming)

        def move(i):
            block = state[i]
            push = f_sum[pl.ds(i, 1), :] * (STEP / SCALE)
            push = jnp.concatenate([push[:, 0:128], push[:, 128:256], push[:, 256:384]], 0)
            velocity = block[3:6] + push / block[7:8]
            position = block[0:3] + STEP * velocity
            if s == steps - 1:
                final[i] = jnp.concatenate([position, velocity], 0)
            else:
                state[i] = jnp.concatenate([position, velocity, block[6:8]], 0)

        each(local, move)


def run_steps(domains, send, pairs, start):
    steps = send.shape[0]
    local = start.shape[0]
    total = local + 2 * GHOSTS
    vmem, smem = (pl.BlockSpec(memory_space=m) for m in (pltpu.VMEM, pltpu.SMEM))
    buffers = []
    for shape in ((GHOSTS, 4, 128), (GHOSTS, 128), (GHOSTS, 128), (GHOSTS, 384)):
        buffers += [pltpu.VMEM((steps, 2) + shape, f32)] * 2
    return pl.pallas_call(
        functools.partial(step_kernel, domains, steps),
        name="steps",
        out_shape=[
            jax.ShapeDtypeStruct((local, 6, 128), f32),
            jax.ShapeDtypeStruct((local, 128), f32),
        ],
        in_specs=[smem, smem, vmem, vmem, vmem],
        out_specs=[vmem, vmem],
        scratch_shapes=[
            pltpu.VMEM((local, 8, 128), f32),
            pltpu.VMEM((total, 8, 128), f32),
            pltpu.VMEM((total, 128), f32),
            pltpu.VMEM((local, 128), f32),
            pltpu.VMEM((local, 128), f32),
            pltpu.VMEM((local, 256, 128), bf16),
            pltpu.VMEM((local, 128, 512), bf16),
            pltpu.VMEM((local, 128), f32),
            pltpu.VMEM((2 * local, 128), f32),
            pltpu.VMEM((local, 384), f32),
            pltpu.VMEM((2 * local, 384), f32),
            pltpu.VMEM((local, 384), f32),
            *buffers,
            pltpu.SemaphoreType.DMA((steps, 4, 2)),
            pltpu.SemaphoreType.DMA((steps, 4, 2)),
        ],
        compiler_params=pltpu.CompilerParams(
            vmem_limit_bytes=67_000_000,
            **(dict(collective_id=1, has_side_effects=True) if domains > 1 else {}),
        ),
    )(send, pairs, send[:, None], pairs[:, None], start)


def pack_kernel(index, pos_vel, entropy, masses, packed, outbox):
    packed[:, 0:6, :] = pos_vel[...]
    packed[:, 6:7, :] = entropy[...]
    packed[:, 7:8, :] = masses[...]

    def one(j):
        outbox[j] = packed[index[j]]

    each(outbox.shape[0], one)


def place_kernel(index, packed, arrived, state):
    half = state.shape[0] // 2

    def stay(j):
        state[j] = packed[index[j]]

    def come(j):
        state[half + j] = arrived[index[half + j]]

    each(half, stay)
    each(half, come)


def call(kernel, name, scalars, operands, outs, scratch=()):
    vmem, smem = (pl.BlockSpec(memory_space=s) for s in (pltpu.VMEM, pltpu.SMEM))
    return pl.pallas_call(
        kernel,
        name=name,
        out_shape=[jax.ShapeDtypeStruct(s, f32) for s in outs],
        in_specs=[smem] * len(scalars) + [vmem] * len(operands),
        out_specs=[vmem] * len(outs),
        scratch_shapes=[pltpu.VMEM(s, f32) for s in scratch],
    )(*scalars, *operands)


def shards(pos_vel, entropy, masses, destination, ghost_send, pair_list):
    devices = lax.axis_size(("dom", "sub"))
    me = lax.axis_index(("dom", "sub"))
    local = pos_vel.shape[0]
    size = pos_vel.shape[2]
    number = jnp.arange(local, dtype=jnp.int32)
    device = jnp.arange(devices, dtype=jnp.int32)
    slot = jnp.arange(devices * MOST, dtype=jnp.int32)
    same = destination[:, None] == destination[None, :]
    rank = jnp.sum((same & (number[:, None] < number[None, :])).astype(jnp.int32), 0)
    staying = destination == me
    out_slot = jnp.where(staying, -1, destination * MOST + rank)
    pack_index = jnp.sum(jnp.where(out_slot[:, None] == slot[None, :], number[:, None], 0), 0)
    shift = (destination - me) % devices
    wanted = (me - device) % devices
    come = jnp.sum((shift[:, None] == wanted[None, :]).astype(jnp.int32), 0)
    come = jnp.where(device == me, 0, come)
    before = jnp.sum(jnp.where(device[:, None] < device[None, :], come[:, None], 0), 0)
    turn = slot % MOST
    source = slot // MOST
    come_at = source[:, None] == device[None, :]
    first = jnp.sum(jnp.where(come_at, before[None, :], 0), 1)
    many = jnp.sum(jnp.where(come_at, come[None, :], 0), 1)
    place = jnp.where(turn < many, first + turn, -1)
    half = local - devices
    stay_index = jnp.sum(
        jnp.where(staying[:, None] & (rank[:, None] == number[None, :half]), number[:, None], 0), 0
    )
    come_index = jnp.sum(jnp.where(place[:, None] == device[None, :], slot[:, None], 0), 0)
    place_index = jnp.concatenate([stay_index, come_index])

    block = (local, 8, size)
    packed, outbox = call(
        pack_kernel, "pack", (pack_index,), (pos_vel, entropy[:, None], masses[:, None]),
        (block, (devices * MOST, 8, size)),
    )
    arrived = lax.all_to_all(
        outbox.reshape(devices, MOST, 8, size), ("dom", "sub"), split_axis=0, concat_axis=0, tiled=True
    ).reshape(devices * MOST, 8, size)
    (state,) = call(place_kernel, "place", (place_index,), (packed, arrived), (block,))
    steps = ghost_send.shape[0]
    return run_steps(lax.axis_size("dom"), ghost_send, pair_list.reshape(steps, -1), state)


def solution(mesh):
    both = ("dom", "sub")
    in_specs = (P(both, None, None), P(both, None), P(both, None), P(both), P(None, both), P(None, both, None))
    out_specs = (P(both, None, None), P(both, None))
    return jax.shard_map(shards, mesh=mesh, in_specs=in_specs, out_specs=out_specs, check_vma=False)
```

time: 318 us -> 194 us (0.61)
  starting transfers between devices: 75.7 us -> 10.4 us
  Pallas kernels: 191 us -> 156 us
  waiting for transfers between devices: 32.2 us -> 13.6 us
  local copies, waits for them, and re-layouts: 15.2 us -> 10.6 us
    pallas_call x10 -> x2, Pallas kernels: 191 us -> 6.43 us  [call(): pl.pallas_call(kernel, name=name, out_shape=[jax.ShapeDtypeStruct(s, f32)...]
    pallas_call x0 -> x1, Pallas kernels: none -> 150 us  [run_steps(): pl.pallas_call(functools.partial(step_kernel, domains, steps), name='step...]
    ppermute x16 -> x0, starting transfers between devices: 65.3 us -> none  [swap(): return (lax.ppermute(high, 'dom', up), lax.ppermute(low, 'dom', down))]
    ppermute x16 -> x0, waiting for transfers between devices: 17 us -> none  [swap(): return (lax.ppermute(high, 'dom', up), lax.ppermute(low, 'dom', down))]
    unnamed x44 -> x13, local copies, waits for them, and re-layouts: 12.2 us -> 6.18 us
  transfers between devices with their start and end apart: 17 -> 1, of which waited for: 17 -> 1; matrix products, arithmetic and copies ran while one was open for 1% -> 2% of each run, Pallas kernels for 0% -> 0%
where the time goes in v2:
time: 194 us
  Pallas kernels  156 us (80%)
  waiting for transfers between devices  13.6 us (7%)
  local copies, waits for them, and re-layouts  10.6 us (5%)
  starting transfers between devices  10.4 us (5%)
  other arithmetic  2.04 us (1%)
    pallas_call x1, Pallas kernels, run_steps(): pl.pallas_call(functools.partial(step_kernel, domains, steps), name='step...  150 us
    all_to_all x1, waiting for transfers between devices, shards(): lax.all_to_all(outbox.reshape(devices, MOST, 8, size), ('dom', 'sub'), sp...  13.6 us
    all_to_all x1, starting transfers between devices, shards(): lax.all_to_all(outbox.reshape(devices, MOST, 8, size), ('dom', 'sub'), sp...  10.4 us
    pallas_call x2, Pallas kernels, call(): pl.pallas_call(kernel, name=name, out_shape=[jax.ShapeDtypeStruct(s, f32)...  6.43 us
    unnamed x13, local copies, waits for them, and re-layouts  6.18 us
  transfers between devices with their start and end apart: 1, of which 1 were waited for; matrix products, arithmetic and copies ran while one was open for 2% of the time, Pallas kernels for 0%

profile of v2, /device:TPU:8, one launch (start us, length us, event | category | flops | bytes accessed | tf_op | source)
XLA Modules:
  0.0 193.9 jit_solution(9053213380173257910)
XLA Ops:
  0.6 0.7 copy-done.2
  1.3 0.1 convert_reduce_fusion
  1.5 0.7 select_reduce_fusion.index
  2.1 2.6 %copy.19.pos_vel = f32[256,6,128]{2,1,0:T(8,128)} copy(f32[256,6,128]{2,0,1:T(8,128)} %param.6) | data formatting | bytes 1572864 | tf_op args[0]
  4.7 3.4 %pack.1 = (f32[256,8,128]{2,1,0:T(8,128)}, f32[256,8,128]{2,1,0:T(8,128)}) custom-call(s32[256]{0:T(256)} %select_reduce_fusion.index, f32[256,6,128]{2,1,0:T(8,128)} %copy.19.pos_vel, f32[256,1,128]{2,1,0:T(1,128)} %bitcast.7, f32[256,1,128]{2,1,0:T(1,128)} %bitcast.8), custom_call_target="tpu_custom_call" | custom-call | tf_op jit(solution)/shard_map/pack/pallas_call | solution.py:415
  8.1 10.4 %all-to-all-start = ((f32[128,2,8,128]{3,2,1,0:T(8,128)}), f32[128,2,8,128]{3,2,1,0:T(8,128)S(1)}, u32[]{:S(2)}, u32[]{:S(2)}) async-start(f32[128,2,8,128]{3,2,1,0:T(8,128)} %bitcast.6), calls=%async_computation | async-start | bytes 2097152 | tf_op jit(solution)/shard_map/all_to_all | solution.py:461
  18.6 0.0 copy-start.3
  18.6 0.1 convert_reduce_fusion.1
  18.7 0.5 copy-done.3
  19.3 0.1 copy.17
  19.4 0.8 broadcast_in_dim_reshape.4.pair_row
  20.2 0.8 reshape.79.pairs
  21.0 0.6 copy-done.4
  21.6 0.1 select_reduce_fusion.5
  21.6 0.2 select_reduce_fusion.2
  21.9 0.6 slice-done
  22.5 0.2 select_reduce_fusion.1
  22.7 0.6 pad_add_fusion.index
  23.3 13.6 %all-to-all-done = f32[128,2,8,128]{3,2,1,0:T(8,128)S(1)} async-done(((f32[128,2,8,128]{3,2,1,0:T(8,128)}), f32[128,2,8,128]{3,2,1,0:T(8,128)S(1)}, u32[]{:S(2)}, u32[]{:S(2)}) %all-to-all-start) | async-done | bytes 1048608 | tf_op jit(solution)/shard_map/all_to_all | solution.py:461
  36.9 1.0 copy-done
  37.9 3.0 %place.1.start = f32[256,8,128]{2,1,0:T(8,128)} custom-call(s32[256]{0:T(256)} %pad_add_fusion.index, f32[256,8,128]{2,1,0:T(8,128)} %get-tuple-element.4.packed, f32[256,8,128]{2,1,0:T(8,128)} %bitcast.5), custom_call_target="tpu_custom_call" | custom-call | tf_op jit(solution)/shard_map/place/pallas_call | solution.py:415
  40.9 150.0 %steps.1 = (f32[256,6,128]{2,1,0:T(8,128)}, f32[256,128]{1,0:T(8,128)}) custom-call(s32[2,128]{1,0:T(2,128)} %send.1, s32[2,512]{1,0:T(2,128)} %reshape.79.pairs, s32[2,1,128]{2,1,0:T(1,128)} %bitcast.9, s32[2,1,512]{2,1,0:T(1,128)} %broadcast_in_dim_reshape.4.pair_row, f32[256,8,128]{2,1,0:T(8,128)} %place.1.start), custom_call_target="tpu_custom_call" | custom-call | tf_op jit(solution)/shard_map/steps/pallas_call | solution.py:356
  190.9 2.3 %copy.21 = f32[256,6,128]{2,0,1:T(8,128)} copy(f32[256,6,128]{2,1,0:T(8,128)} %get-tuple-element.10) | data formatting | bytes 1572864 | tf_op jit(solution)/shard_map/steps/pallas_call | solution.py:356
  193.2 0.7 copy.23
  (13 shorter events, 0.1 us)
Async XLA Ops:
  0.6 0.7 copy-start.2
  8.1 28.8 %all-to-all-start = ((f32[128,2,8,128]{3,2,1,0:T(8,128)}), f32[128,2,8,128]{3,2,1,0:T(8,128)S(1)}, u32[]{:S(2)}, u32[]{:S(2)}) async-start(f32[128,2,8,128]{3,2,1,0:T(8,128)} %bitcast.6), calls=%async_computation | async-start | bytes 2097152 | tf_op jit(solution)/shard_map/all_to_all | solution.py:461
  18.6 0.7 copy-start.3
  21.0 0.6 copy-start.4
  21.9 0.6 slice-start
  36.9 1.0 copy-start
  190.9 2.3 %copy-start.1 = (f32[256,128]{1,0:T(8,128)S(1)}, f32[256,128]{1,0:T(8,128)}, u32[]{:S(2)}) copy-start(f32[256,128]{1,0:T(8,128)} %get-tuple-element.21) | copy-start | bytes 393220

commit v3 on v2

--- a/solution.py
+++ b/solution.py
@@ -230,7 +230,7 @@
             own_m[i, 0:128] = h
             own_m[i, 128:256] = l
 
-        each(local, own_density, UNROLL)
+        each(local, own_density, 32)
         if domains > 1:
             finish(s, 0, p_out, p_in)
 
@@ -254,12 +254,16 @@
             sums = column_sum(m)
             r_pair[pl.ds(2 * i, 1), :] = sums[:, :128]
             r_pair[pl.ds(2 * i + 1, 1), :] = sums[:, 128:]
-            r_own[pl.ds(i, 1), :] += column_sum((m[:, :128] + m[:, 128:]).T)
+            back = jnp.concatenate(split2(m[:, :128] + m[:, 128:]), 1)
+            back = lax.dot_general(
+                jnp.ones((8, 256), bf16), back, (((1,), (1,)), ((), ())), preferred_element_type=f32
+            )
+            r_own[pl.ds(i, 1), :] += back[0:1]
             h, l = split2(m)
             pair_m[i, :, 0:256] = h
             pair_m[i, :, 256:512] = l
 
-        each(local, pair_density, UNROLL)
+        each(local, pair_density, 16)
         chosen = pair_row[s]
         sent = send_row[s]
         for side in range(2):
@@ -292,7 +296,7 @@
             )
             f_own[pl.ds(i, 1), :] = lanes(force_rows(v, y))
 
-        each(local, own_force, UNROLL)
+        each(local, own_force, 32)
         if domains > 1:
             finish(s, 2, q_out, q_in)
         press[local : local + GHOSTS] = q_in[s, 0]
@@ -319,7 +323,7 @@
             f_pair[pl.ds(2 * i, 1), :] = lanes(force_rows(vs[1], down[:, :128]))
             f_pair[pl.ds(2 * i + 1, 1), :] = lanes(force_rows(vs[2], down[:, 128:]))
 
-        each(local, pair_force, UNROLL)
+        each(local, pair_force, 32)
         for side in range(2):
             f_out[s, side] = routed_sum(chosen, local + side * GHOSTS, GHOSTS, f_pair[...])
         for part in range(0, local, 128):
@@ -338,7 +342,9 @@
             velocity = block[3:6] + push / block[7:8]
             position = block[0:3] + STEP * velocity
             if s == steps - 1:
-                final[i] = jnp.concatenate([position, velocity], 0)
+                for c in range(3):
+                    final[c, pl.ds(i, 1), :] = position[c : c + 1]
+                    final[3 + c, pl.ds(i, 1), :] = velocity[c : c + 1]
             else:
                 state[i] = jnp.concatenate([position, velocity, block[6:8]], 0)
 
@@ -357,7 +363,7 @@
         functools.partial(step_kernel, domains, steps),
         name="steps",
         out_shape=[
-            jax.ShapeDtypeStruct((local, 6, 128), f32),
+            jax.ShapeDtypeStruct((6, local, 128), f32),
             jax.ShapeDtypeStruct((local, 128), f32),
         ],
         in_specs=[smem, smem, vmem, vmem, vmem],
@@ -386,84 +392,127 @@
     )(send, pairs, send[:, None], pairs[:, None], start)
 
 
-def pack_kernel(index, pos_vel, entropy, masses, packed, outbox):
-    packed[:, 0:6, :] = pos_vel[...]
-    packed[:, 6:7, :] = entropy[...]
-    packed[:, 7:8, :] = masses[...]
-
-    def one(j):
-        outbox[j] = packed[index[j]]
-
-    each(outbox.shape[0], one)
-
-
-def place_kernel(index, packed, arrived, state):
-    half = state.shape[0] // 2
+def migrate_kernel(
+    devices, pack_index, place_index, pos_vel, entropy, masses, state, packed, outbox, inbox, send_sem, recv_sem
+):
+    subs = lax.axis_size("sub")
+    me = lax.axis_index("dom") * subs + lax.axis_index("sub")
+
+    def device(k):
+        there = lax.rem(me + k, devices)
+        return {"dom": there // subs, "sub": lax.rem(there, subs)}
+
+    mesh_id = pl.DeviceIdType.MESH
+    barrier = pltpu.get_barrier_semaphore()
+
+    def greet(k, _):
+        pl.semaphore_signal(barrier, inc=1, device_id=device(k), device_id_type=mesh_id)
+        return 0
+
+    lax.fori_loop(1, devices, greet, 0)
+    local = packed.shape[0]
+
+    def gather(g):
+        rows = pl.ds(pl.multiple_of(g * 8, 8), 8)
+        for c in range(6):
+            packed[rows, c, :] = pos_vel[c, rows, :]
+        packed[rows, 6, :] = entropy[rows, :]
+        packed[rows, 7, :] = masses[rows, :]
+
+    each(local // 8, gather, 4)
+
+    def pack(k):
+        for r in range(MOST):
+            outbox[k, r] = packed[pack_index[k * MOST + r]]
+
+    each(devices, pack)
+    pl.semaphore_wait(barrier, devices - 1)
+
+    def copy(source, target, k):
+        return pltpu.make_async_remote_copy(
+            src_ref=source, dst_ref=target, send_sem=send_sem, recv_sem=recv_sem,
+            device_id=device(k), device_id_type=mesh_id,
+        )
+
+    def send(j, _):
+        k = lax.rem(j * 45, devices)
+        copy(outbox.at[k], inbox.at[k], k).start()
+        return 0
+
+    lax.fori_loop(1, devices, send, 0)
+    half = local // 2
 
     def stay(j):
-        state[j] = packed[index[j]]
+        state[j] = packed[place_index[j]]
+
+    each(half, stay)
+    everything = pl.ds(1, devices - 1)
+    whole = copy(outbox.at[everything], inbox.at[everything], 1)
+    whole.wait_send()
+    whole.wait_recv()
 
     def come(j):
-        state[half + j] = arrived[index[half + j]]
-
-    each(half, stay)
+        slot = place_index[half + j]
+        state[half + j] = inbox[slot // MOST, lax.rem(slot, MOST)]
+
     each(half, come)
 
 
-def call(kernel, name, scalars, operands, outs, scratch=()):
-    vmem, smem = (pl.BlockSpec(memory_space=s) for s in (pltpu.VMEM, pltpu.SMEM))
+def migrate(devices, pack_index, place_index, pos_vel, entropy, masses):
+    local, size = entropy.shape
+    vmem, smem = (pl.BlockSpec(memory_space=m) for m in (pltpu.VMEM, pltpu.SMEM))
+    block = (local, 8, size)
     return pl.pallas_call(
-        kernel,
-        name=name,
-        out_shape=[jax.ShapeDtypeStruct(s, f32) for s in outs],
-        in_specs=[smem] * len(scalars) + [vmem] * len(operands),
-        out_specs=[vmem] * len(outs),
-        scratch_shapes=[pltpu.VMEM(s, f32) for s in scratch],
-    )(*scalars, *operands)
+        functools.partial(migrate_kernel, devices),
+        name="migrate",
+        out_shape=jax.ShapeDtypeStruct(block, f32),
+        in_specs=[smem, smem, vmem, vmem, vmem],
+        out_specs=vmem,
+        scratch_shapes=[
+            pltpu.VMEM(block, f32),
+            pltpu.VMEM((devices, MOST, 8, size), f32),
+            pltpu.VMEM((devices, MOST, 8, size), f32),
+            pltpu.SemaphoreType.DMA,
+            pltpu.SemaphoreType.DMA,
+        ],
+        compiler_params=pltpu.CompilerParams(collective_id=2, has_side_effects=True),
+    )(pack_index, place_index, pos_vel, entropy, masses)
 
 
 def shards(pos_vel, entropy, masses, destination, ghost_send, pair_list):
     devices = lax.axis_size(("dom", "sub"))
     me = lax.axis_index(("dom", "sub"))
     local = pos_vel.shape[0]
-    size = pos_vel.shape[2]
     number = jnp.arange(local, dtype=jnp.int32)
     device = jnp.arange(devices, dtype=jnp.int32)
     slot = jnp.arange(devices * MOST, dtype=jnp.int32)
     same = destination[:, None] == destination[None, :]
     rank = jnp.sum((same & (number[:, None] < number[None, :])).astype(jnp.int32), 0)
     staying = destination == me
-    out_slot = jnp.where(staying, -1, destination * MOST + rank)
+    shift = (destination - me) % devices
+    out_slot = jnp.where(staying, -1, shift * MOST + rank)
     pack_index = jnp.sum(jnp.where(out_slot[:, None] == slot[None, :], number[:, None], 0), 0)
-    shift = (destination - me) % devices
-    wanted = (me - device) % devices
-    come = jnp.sum((shift[:, None] == wanted[None, :]).astype(jnp.int32), 0)
-    come = jnp.where(device == me, 0, come)
-    before = jnp.sum(jnp.where(device[:, None] < device[None, :], come[:, None], 0), 0)
-    turn = slot % MOST
-    source = slot // MOST
-    come_at = source[:, None] == device[None, :]
-    first = jnp.sum(jnp.where(come_at, before[None, :], 0), 1)
-    many = jnp.sum(jnp.where(come_at, come[None, :], 0), 1)
-    place = jnp.where(turn < many, first + turn, -1)
+    source = (me - device) % devices
+    come = jnp.sum((shift[:, None] == device[None, :]).astype(jnp.int32), 0)
+    come = jnp.where(device == 0, 0, come)
+    before = jnp.sum(jnp.where(source[:, None] < source[None, :], come[:, None], 0), 0)
     half = local - devices
     stay_index = jnp.sum(
         jnp.where(staying[:, None] & (rank[:, None] == number[None, :half]), number[:, None], 0), 0
     )
-    come_index = jnp.sum(jnp.where(place[:, None] == device[None, :], slot[:, None], 0), 0)
+    come_index = sum(
+        jnp.sum(
+            jnp.where((before[:, None] + r == device[None, :]) & (come[:, None] > r), device[:, None] * MOST + r, 0), 0
+        )
+        for r in range(MOST)
+    )
     place_index = jnp.concatenate([stay_index, come_index])
-
-    block = (local, 8, size)
-    packed, outbox = call(
-        pack_kernel, "pack", (pack_index,), (pos_vel, entropy[:, None], masses[:, None]),
-        (block, (devices * MOST, 8, size)),
+    state = migrate(
+        devices, pack_index, place_index, jnp.transpose(pos_vel, (1, 0, 2)), entropy, masses
     )
-    arrived = lax.all_to_all(
-        outbox.reshape(devices, MOST, 8, size), ("dom", "sub"), split_axis=0, concat_axis=0, tiled=True
-    ).reshape(devices * MOST, 8, size)
-    (state,) = call(place_kernel, "place", (place_index,), (packed, arrived), (block,))
     steps = ghost_send.shape[0]
-    return run_steps(lax.axis_size("dom"), ghost_send, pair_list.reshape(steps, -1), state)
+    final, density = run_steps(lax.axis_size("dom"), ghost_send, pair_list.reshape(steps, -1), state)
+    return jnp.transpose(final, (1, 0, 2)), density
 
 
 def solution(mesh):

time: 194 us -> 147 us (0.76)
  Pallas kernels: 156 us -> 138 us
  waiting for transfers between devices: 13.6 us -> 0 us
  starting transfers between devices: 10.4 us -> 0 us
  local copies, waits for them, and re-layouts: 10.6 us -> 6.32 us
    pallas_call x1, Pallas kernels: 150 us -> 110 us  [run_steps(): pl.pallas_call(functools.partial(step_kernel, domains, steps), name='step...]
    pallas_call x2 -> x1, Pallas kernels: 6.43 us -> 27.4 us  [migrate(): pl.pallas_call(functools.partial(migrate_kernel, devices), name='migrate'...]
    all_to_all x1 -> x0, waiting for transfers between devices: 13.6 us -> none  [shards(): lax.all_to_all(outbox.reshape(devices, MOST, 8, size), ('dom', 'sub'), sp...]
    all_to_all x1 -> x0, starting transfers between devices: 10.4 us -> none  [shards(): lax.all_to_all(outbox.reshape(devices, MOST, 8, size), ('dom', 'sub'), sp...]
    pallas_call x1 -> x0, local copies, waits for them, and re-layouts: 2.29 us -> none  [run_steps(): pl.pallas_call(functools.partial(step_kernel, domains, steps), name='step...]
    unnamed x13 -> x11, local copies, waits for them, and re-layouts: 6.18 us -> 4.13 us
  transfers between devices with their start and end apart: 1 -> 0, of which waited for: 1 -> 0; matrix products, arithmetic and copies ran while one was open for 2% -> 0% of each run, Pallas kernels for 0% -> 0%
where the time goes in v3:
time: 147 us
  Pallas kernels  138 us (94%)
  local copies, waits for them, and re-layouts  6.32 us (4%)
  other arithmetic  2.03 us (1%)
    pallas_call x1, Pallas kernels, run_steps(): pl.pallas_call(functools.partial(step_kernel, domains, steps), name='step...  110 us
    pallas_call x1, Pallas kernels, migrate(): pl.pallas_call(functools.partial(migrate_kernel, devices), name='migrate'...  27.4 us
    unnamed x11, local copies, waits for them, and re-layouts  4.13 us

profile of v3, /device:TPU:8, one launch (start us, length us, event | category | flops | bytes accessed | tf_op | source)
XLA Modules:
  0.0 147.0 jit_solution(16150130370570889972)
XLA Ops:
  0.7 0.0 copy-start.1
  0.7 0.7 copy-done.1
  1.3 0.1 convert_reduce_fusion
  1.5 0.0 copy-start.3
  1.5 0.6 copy-done.3
  2.0 0.0 slice-start
  2.1 0.6 slice-done
  2.7 0.2 convert_reduce_fusion.1
  2.9 0.7 select_reduce_fusion.pack_index
  3.6 0.1 select_reduce_fusion.4
  3.7 0.1 select_reduce_fusion.3
  3.9 0.0 copy-start.2
  3.9 0.1 select_reduce_fusion.2
  4.0 0.6 pad_add_fusion.place_index
  4.6 0.0 copy-done.2
  4.6 0.1 copy.13
  4.8 0.8 broadcast_in_dim_reshape.4.pair_row
  5.6 0.8 reshape.76.pairs
  6.3 27.4 %migrate.1.start = f32[256,8,128]{2,1,0:T(8,128)} custom-call(s32[256]{0:T(256)} %select_reduce_fusion.pack_index, s32[256]{0:T(256)} %pad_add_fusion.place_index, f32[6,256,128]{2,1,0:T(8,128)} %bitcast.3, f32[256,128]{1,0:T(8,128)} %entropy.1, f32[256,128]{1,0:T(8,128)} %masses.1), custom_call_target="tpu_custom_call" | custom-call | tf_op jit(solution)/shard_map/migrate/pallas_call | solution.py:465
  33.7 110.5 %steps.1 = (f32[6,256,128]{2,1,0:T(8,128)}, f32[256,128]{1,0:T(8,128)}) custom-call(s32[2,128]{1,0:T(2,128)} %send.1, s32[2,512]{1,0:T(2,128)} %reshape.76.pairs, s32[2,1,128]{2,1,0:T(1,128)} %bitcast.5, s32[2,1,512]{2,1,0:T(1,128)} %broadcast_in_dim_reshape.4.pair_row, f32[256,8,128]{2,1,0:T(8,128)} %migrate.1.start), custom_call_target="tpu_custom_call" | custom-call | tf_op jit(solution)/shard_map/steps/pallas_call | solution.py:362
  144.2 0.0 copy-start
  144.2 2.1 %copy.18 = f32[256,6,128]{2,0,1:T(8,128)} copy(f32[256,6,128]{2,0,1:T(8,128)} %bitcast.4) | data formatting | bytes 1572864
  146.3 0.0 copy-done
  146.3 0.7 copy.19
  (9 shorter events, 0.1 us)
Async XLA Ops:
  0.7 0.7 copy-start.1
  1.5 0.6 copy-start.3
  2.0 0.7 slice-start
  3.9 0.8 copy-start.2
  144.2 2.1 %copy-start = (f32[256,128]{1,0:T(8,128)S(1)}, f32[256,128]{1,0:T(8,128)}, u32[]{:S(2)}) copy-start(f32[256,128]{1,0:T(8,128)} %get-tuple-element.16) | copy-start | bytes 393220

commit v4 on v3

--- a/solution.py
+++ b/solution.py
@@ -36,29 +36,13 @@
 
 
 def left_rows(moved, row):
-    h, m, l = split3(moved)
-    one = jnp.where(row == 4, 1.0, 0.0)
-    a1 = jnp.where(row < 4, h, one)
-    a2 = jnp.where(row < 3, h, jnp.where(row == 3, m, one))
-    a3 = jnp.where(row < 3, m, jnp.where(row == 3, l, one))
-    a4 = jnp.where(row < 3, m, 0.0)
-    a5 = jnp.where(row < 3, h, 0.0)
-    a6 = jnp.where(row < 3, l, 0.0)
-    return jnp.concatenate([a1, a2, a3, a4, a5, a6], 0).astype(bf16)
+    h, m, l = split3(jnp.where(row == 4, 1.0, moved))
+    return jnp.concatenate([h, h, m, m, h, l], 0).astype(bf16)
 
 
 def right_rows(moved, row):
-    h, m, l = split3(moved)
-    one = jnp.where(row == 3, 1.0, 0.0)
-    low = row < 3
-    four = row == 4
-    b1 = jnp.where(low | four, h, one)
-    b2 = jnp.where(low | four, m, one)
-    b3 = jnp.where(low, h, jnp.where(four, l, one))
-    b4 = jnp.where(low, m, 0.0)
-    b5 = jnp.where(low, l, 0.0)
-    b6 = jnp.where(low, h, 0.0)
-    return jnp.concatenate([b1, b2, b3, b4, b5, b6], 0).astype(bf16)
+    h, m, l = split3(jnp.where(row == 3, 1.0, moved))
+    return jnp.concatenate([h, m, h, m, l, h], 0).astype(bf16)
 
 
 def centre_of(block, row):
@@ -129,11 +113,14 @@
 
 
 def step_kernel(
-    domains, steps, send, pairs, send_row, pair_row, start, final, density,
-    state, blocks, press, entropy, masses, own_m, pair_m, r_own, r_pair, f_own, f_pair, f_sum,
-    p_out, p_in, r_out, r_in, q_out, q_in, f_out, f_in, send_sem, recv_sem,
+    domains, subs, steps, pack_index, place_index, send, pairs, send_row, pair_row,
+    pos_vel, entropy_in, masses_in, final, density, outbox, inbox, state, blocks, press, entropy, masses, own_m, pair_m, r_own, r_pair, f_own, f_pair, f_sum,
+    p_out, p_in, r_out, r_in, q_out, q_in, f_out, f_in, send_sem, recv_sem, move_sems,
 ):
-    local = start.shape[0]
+    local = state.shape[0]
+    half = local // 2
+    devices = domains * subs
+    several = devices > 1
     total = local + 2 * GHOSTS
     dom = lax.axis_index("dom")
     has_low, has_high = dom > 0, dom < domains - 1
@@ -170,16 +157,38 @@
             to_high.wait_send()
             to_low.wait_recv()
 
-    if domains > 1:
+    me = dom * subs + lax.axis_index("sub")
+    mesh_id = pl.DeviceIdType.MESH
+
+    def device(k):
+        there = lax.rem(me + k, devices)
+        return {"dom": there // subs, "sub": lax.rem(there, subs)}
+
+    if several:
         barrier = pltpu.get_barrier_semaphore()
 
-        def greet(target):
-            pl.semaphore_signal(
-                barrier, inc=1, device_id={"dom": target}, device_id_type=pl.DeviceIdType.MESH
-            )
-
-        pl.when(has_low)(lambda: greet(dom - 1))
-        pl.when(has_high)(lambda: greet(dom + 1))
+        def greet(k, _):
+            pl.semaphore_signal(barrier, inc=1, device_id=device(k), device_id_type=mesh_id)
+            return 0
+
+        lax.fori_loop(1, devices, greet, 0)
+
+    packed = blocks
+
+    def gather(g):
+        rows = pl.ds(pl.multiple_of(g * 8, 8), 8)
+        for c in range(6):
+            packed[rows, c, :] = pos_vel[c, rows, :]
+        packed[rows, 6, :] = entropy_in[rows, :]
+        packed[rows, 7, :] = masses_in[rows, :]
+
+    each(local // 8, gather, 4)
+
+    def pack(k):
+        for r in range(MOST):
+            outbox[k, r] = packed[pack_index[k * MOST + r]]
+
+    each(devices, pack)
 
     for side, has in ((0, has_low), (1, has_high)):
 
@@ -192,45 +201,76 @@
                 for into in (r_in, q_in, f_in):
                     into[s, side] = jnp.zeros(into.shape[2:], f32)
 
-    def enter(i):
-        block = start[i]
+    def copy(source, target, k):
+        return pltpu.make_async_remote_copy(
+            src_ref=source, dst_ref=target, send_sem=move_sems.at[0], recv_sem=move_sems.at[1],
+            device_id=device(k), device_id_type=mesh_id,
+        )
+
+    if several:
+        pl.semaphore_wait(barrier, devices - 1)
+
+        def send_moving(j, _):
+            k = lax.rem(j * 45, devices)
+            copy(outbox.at[k], inbox.at[k], k).start()
+            return 0
+
+        lax.fori_loop(1, devices, send_moving, 0)
+
+    def enter(i, block):
         state[i] = block
         entropy[pl.ds(i, 1), :] = block[6:7]
         masses[pl.ds(i, 1), :] = block[7:8]
 
-    each(local, enter)
+    def scaled(i):
+        block = state[i]
+        level = jnp.log2(block[7:8])
+        blocks[i] = jnp.concatenate(
+            [block[0:3] * SCALE, level, level, jnp.zeros((3, 128), f32)], 0
+        )
+
+    def own_density(i):
+        block = blocks[i]
+        block = features(block, centre_of(block, row), row)
+        m = weights_of(block, (block,), row)
+        r_own[pl.ds(i, 1), :] = column_sum(m)
+        h, l = split2(m)
+        own_m[i, 0:128] = h
+        own_m[i, 128:256] = l
+
+    each(half, lambda j: enter(j, packed[place_index[j]]))
+    each(half, scaled)
+    each(half, own_density, 32)
+    if several:
+        everything = pl.ds(1, devices - 1)
+        whole = copy(outbox.at[everything], inbox.at[everything], 1)
+        whole.wait_send()
+        whole.wait_recv()
+
+    def come(j):
+        slot = place_index[half + j]
+        enter(half + j, inbox[slot // MOST, lax.rem(slot, MOST)])
+        scaled(half + j)
+
+    each(half, come)
 
     for s in range(steps):
 
-        def scaled(i):
-            block = state[i]
-            level = jnp.log2(block[7:8])
-            blocks[i] = jnp.concatenate(
-                [block[0:3] * SCALE, level, level, jnp.zeros((3, 128), f32)], 0
-            )
-
-        each(local, scaled)
+        if s > 0:
+            each(local, scaled)
 
         def pick(j):
             for side in range(2):
                 p_out[s, side, j] = blocks[send[s, side * GHOSTS + j]][0:4]
 
         each(GHOSTS, pick)
-        if s == 0 and domains > 1:
-            pl.semaphore_wait(barrier, has_low.astype(jnp.int32) + has_high.astype(jnp.int32))
         if domains > 1:
             begin(s, 0, p_out, p_in)
 
-        def own_density(i):
-            block = blocks[i]
-            block = features(block, centre_of(block, row), row)
-            m = weights_of(block, (block,), row)
-            r_own[pl.ds(i, 1), :] = column_sum(m)
-            h, l = split2(m)
-            own_m[i, 0:128] = h
-            own_m[i, 128:256] = l
-
-        each(local, own_density, 32)
+        if s == 0:
+            each(local - half, lambda j: own_density(half + j), 32)
+        else:
+            each(local, own_density, 32)
         if domains > 1:
             finish(s, 0, p_out, p_in)
 
@@ -248,12 +288,12 @@
             centre = centre_of(block, row)
             own, first, second = (
                 features(b, centre, row)
-                for b in (block, blocks[pairs[s, 2 * i]], blocks[pairs[s, 2 * i + 1]])
+                for b in (block, blocks[pairs[s, 0, i]], blocks[pairs[s, 1, i]])
             )
             m = weights_of(own, (first, second), row)
             sums = column_sum(m)
-            r_pair[pl.ds(2 * i, 1), :] = sums[:, :128]
-            r_pair[pl.ds(2 * i + 1, 1), :] = sums[:, 128:]
+            r_pair[pl.ds(i, 1), :] = sums[:, :128]
+            r_pair[pl.ds(local + i, 1), :] = sums[:, 128:]
             back = jnp.concatenate(split2(m[:, :128] + m[:, 128:]), 1)
             back = lax.dot_general(
                 jnp.ones((8, 256), bf16), back, (((1,), (1,)), ((), ())), preferred_element_type=f32
@@ -263,9 +303,9 @@
             pair_m[i, :, 0:256] = h
             pair_m[i, :, 256:512] = l
 
-        each(local, pair_density, 16)
-        chosen = pair_row[s]
-        sent = send_row[s]
+        each(local, pair_density, 32)
+        chosen = jnp.concatenate([pair_row[s, 0:1], pair_row[s, 1:2]], 1)
+        sent = send_row[s : s + 1, :]
         for side in range(2):
             r_out[s, side] = routed_sum(chosen, local + side * GHOSTS, GHOSTS, r_pair[...])
         for part in range(0, local, 128):
@@ -305,7 +345,7 @@
         def pair_force(i):
             block = blocks[i]
             centre = centre_of(block, row)
-            n1, n2 = pairs[s, 2 * i], pairs[s, 2 * i + 1]
+            n1, n2 = pairs[s, 0, i], pairs[s, 1, i]
             vs = [
                 vector_rows(b - centre, press[pl.ds(n, 1), :])
                 for b, n in ((block, i), (blocks[n1], n1), (blocks[n2], n2))
@@ -320,8 +360,8 @@
             down = join(
                 jnp.dot(jnp.concatenate([own, own], 1), stacked, preferred_element_type=f32)
             )
-            f_pair[pl.ds(2 * i, 1), :] = lanes(force_rows(vs[1], down[:, :128]))
-            f_pair[pl.ds(2 * i + 1, 1), :] = lanes(force_rows(vs[2], down[:, 128:]))
+            f_pair[pl.ds(i, 1), :] = lanes(force_rows(vs[1], down[:, :128]))
+            f_pair[pl.ds(local + i, 1), :] = lanes(force_rows(vs[2], down[:, 128:]))
 
         each(local, pair_force, 32)
         for side in range(2):
@@ -351,24 +391,27 @@
         each(local, move)
 
 
-def run_steps(domains, send, pairs, start):
+def run_steps(domains, subs, pack_index, place_index, send, pairs, pos_vel, entropy, masses):
     steps = send.shape[0]
-    local = start.shape[0]
+    local = pos_vel.shape[1]
+    devices = domains * subs
     total = local + 2 * GHOSTS
     vmem, smem = (pl.BlockSpec(memory_space=m) for m in (pltpu.VMEM, pltpu.SMEM))
     buffers = []
     for shape in ((GHOSTS, 4, 128), (GHOSTS, 128), (GHOSTS, 128), (GHOSTS, 384)):
         buffers += [pltpu.VMEM((steps, 2) + shape, f32)] * 2
     return pl.pallas_call(
-        functools.partial(step_kernel, domains, steps),
+        functools.partial(step_kernel, domains, subs, steps),
         name="steps",
         out_shape=[
             jax.ShapeDtypeStruct((6, local, 128), f32),
             jax.ShapeDtypeStruct((local, 128), f32),
         ],
-        in_specs=[smem, smem, vmem, vmem, vmem],
+        in_specs=[smem] * 4 + [vmem] * 5,
         out_specs=[vmem, vmem],
         scratch_shapes=[
+            pltpu.VMEM((devices, MOST, 8, 128), f32),
+            pltpu.VMEM((devices, MOST, 8, 128), f32),
             pltpu.VMEM((local, 8, 128), f32),
             pltpu.VMEM((total, 8, 128), f32),
             pltpu.VMEM((total, 128), f32),
@@ -384,99 +427,13 @@
             *buffers,
             pltpu.SemaphoreType.DMA((steps, 4, 2)),
             pltpu.SemaphoreType.DMA((steps, 4, 2)),
+            pltpu.SemaphoreType.DMA((2,)),
         ],
         compiler_params=pltpu.CompilerParams(
             vmem_limit_bytes=67_000_000,
-            **(dict(collective_id=1, has_side_effects=True) if domains > 1 else {}),
+            **(dict(collective_id=1, has_side_effects=True) if devices > 1 else {}),
         ),
-    )(send, pairs, send[:, None], pairs[:, None], start)
-
-
-def migrate_kernel(
-    devices, pack_index, place_index, pos_vel, entropy, masses, state, packed, outbox, inbox, send_sem, recv_sem
-):
-    subs = lax.axis_size("sub")
-    me = lax.axis_index("dom") * subs + lax.axis_index("sub")
-
-    def device(k):
-        there = lax.rem(me + k, devices)
-        return {"dom": there // subs, "sub": lax.rem(there, subs)}
-
-    mesh_id = pl.DeviceIdType.MESH
-    barrier = pltpu.get_barrier_semaphore()
-
-    def greet(k, _):
-        pl.semaphore_signal(barrier, inc=1, device_id=device(k), device_id_type=mesh_id)
-        return 0
-
-    lax.fori_loop(1, devices, greet, 0)
-    local = packed.shape[0]
-
-    def gather(g):
-        rows = pl.ds(pl.multiple_of(g * 8, 8), 8)
-        for c in range(6):
-            packed[rows, c, :] = pos_vel[c, rows, :]
-        packed[rows, 6, :] = entropy[rows, :]
-        packed[rows, 7, :] = masses[rows, :]
-
-    each(local // 8, gather, 4)
-
-    def pack(k):
-        for r in range(MOST):
-            outbox[k, r] = packed[pack_index[k * MOST + r]]
-
-    each(devices, pack)
-    pl.semaphore_wait(barrier, devices - 1)
-
-    def copy(source, target, k):
-        return pltpu.make_async_remote_copy(
-            src_ref=source, dst_ref=target, send_sem=send_sem, recv_sem=recv_sem,
-            device_id=device(k), device_id_type=mesh_id,
-        )
-
-    def send(j, _):
-        k = lax.rem(j * 45, devices)
-        copy(outbox.at[k], inbox.at[k], k).start()
-        return 0
-
-    lax.fori_loop(1, devices, send, 0)
-    half = local // 2
-
-    def stay(j):
-        state[j] = packed[place_index[j]]
-
-    each(half, stay)
-    everything = pl.ds(1, devices - 1)
-    whole = copy(outbox.at[everything], inbox.at[everything], 1)
-    whole.wait_send()
-    whole.wait_recv()
-
-    def come(j):
-        slot = place_index[half + j]
-        state[half + j] = inbox[slot // MOST, lax.rem(slot, MOST)]
-
-    each(half, come)
-
-
-def migrate(devices, pack_index, place_index, pos_vel, entropy, masses):
-    local, size = entropy.shape
-    vmem, smem = (pl.BlockSpec(memory_space=m) for m in (pltpu.VMEM, pltpu.SMEM))
-    block = (local, 8, size)
-    return pl.pallas_call(
-        functools.partial(migrate_kernel, devices),
-        name="migrate",
-        out_shape=jax.ShapeDtypeStruct(block, f32),
-        in_specs=[smem, smem, vmem, vmem, vmem],
-        out_specs=vmem,
-        scratch_shapes=[
-            pltpu.VMEM(block, f32),
-            pltpu.VMEM((devices, MOST, 8, size), f32),
-            pltpu.VMEM((devices, MOST, 8, size), f32),
-            pltpu.SemaphoreType.DMA,
-            pltpu.SemaphoreType.DMA,
-        ],
-        compiler_params=pltpu.CompilerParams(collective_id=2, has_side_effects=True),
-    )(pack_index, place_index, pos_vel, entropy, masses)
+    )(pack_index, place_index, send, pairs, send, pairs, pos_vel, entropy, masses)
 
 
 def shards(pos_vel, entropy, masses, destination, ghost_send, pair_list):
@@ -507,11 +464,10 @@
         for r in range(MOST)
     )
     place_index = jnp.concatenate([stay_index, come_index])
-    state = migrate(
-        devices, pack_index, place_index, jnp.transpose(pos_vel, (1, 0, 2)), entropy, masses
+    final, density = run_steps(
+        lax.axis_size("dom"), lax.axis_size("sub"), pack_index, place_index, ghost_send,
+        jnp.transpose(pair_list, (0, 2, 1)), jnp.transpose(pos_vel, (1, 0, 2)), entropy, masses,
     )
-    steps = ghost_send.shape[0]
-    final, density = run_steps(lax.axis_size("dom"), ghost_send, pair_list.reshape(steps, -1), state)
     return jnp.transpose(final, (1, 0, 2)), density
 
 

time: 147 us -> 134 us (0.912)
  Pallas kernels: 138 us -> 126 us
  local copies, waits for them, and re-layouts: 6.32 us -> 4.63 us
    pallas_call x2 -> x1, Pallas kernels: 138 us -> 126 us  [run_steps(): pl.pallas_call(functools.partial(step_kernel, domains, subs, steps), name...]
    unnamed x11 -> x8, local copies, waits for them, and re-layouts: 4.13 us -> 3.98 us
where the time goes in v4:
time: 134 us; the launch traced here: 133 us
  Pallas kernels  126 us (94%)
  local copies, waits for them, and re-layouts  4.63 us (3%)
  other arithmetic  1.98 us (1%)
    pallas_call x1, Pallas kernels, run_steps(): pl.pallas_call(functools.partial(step_kernel, domains, subs, steps), name...  126 us
    unnamed x8, local copies, waits for them, and re-layouts  3.98 us

profile of v4, /device:TPU:8, one launch (start us, length us, event | category | flops | bytes accessed | tf_op | source)
XLA Modules:
  0.0 133.4 jit_solution(16953260095595678159)
XLA Ops:
  0.7 0.0 copy-start.1
  0.7 0.7 copy-done.1
  1.3 0.1 convert_reduce_fusion
  1.5 0.0 copy-start.2
  1.5 0.6 copy-done.2
  2.0 0.0 slice-start
  2.1 0.6 slice-done
  2.7 0.2 convert_reduce_fusion.1
  2.9 0.7 select_reduce_fusion.pack_index
  3.6 0.1 select_reduce_fusion.4
  3.7 0.1 select_reduce_fusion.3
  3.8 0.1 select_reduce_fusion.2
  4.0 0.6 pad_add_fusion.place_index
  4.6 126.1 %steps.1 = (f32[6,256,128]{2,1,0:T(8,128)}, f32[256,128]{1,0:T(8,128)}) custom-call(s32[256]{0:T(256)} %select_reduce_fusion.pack_index, s32[256]{0:T(256)} %pad_add_fusion.place_index, s32[2,128]{1,0:T(2,128)} %send_row.1, s32[2,2,256]{2,1,0:T(2,128)} %bitcast.5, s32[2,128]{1,0:T(2,128)} %send_row.1, s32[2,2,256]{2,1,0:T(2,128)} %bitcast.6, ...), custom_call_target="tpu_custom_call" | custom-call | tf_op jit(solution)/shard_map/steps/pallas_call | solution.py:403
  130.7 0.0 copy-start
  130.7 2.1 %copy.10 = f32[256,6,128]{2,0,1:T(8,128)} copy(f32[256,6,128]{2,0,1:T(8,128)} %bitcast.3) | data formatting | bytes 1572864
  132.8 0.0 copy-done
  132.8 0.7 copy.11
  (9 shorter events, 0.1 us)
Async XLA Ops:
  0.7 0.7 copy-start.1
  1.5 0.6 copy-start.2
  2.0 0.7 slice-start
  130.7 2.1 %copy-start = (f32[256,128]{1,0:T(8,128)S(1)}, f32[256,128]{1,0:T(8,128)}, u32[]{:S(2)}) copy-start(f32[256,128]{1,0:T(8,128)} %get-tuple-element.16) | copy-start | bytes 393220

commit v5 on v4

--- a/solution.py
+++ b/solution.py
@@ -240,7 +240,7 @@
 
     each(half, lambda j: enter(j, packed[place_index[j]]))
     each(half, scaled)
-    each(half, own_density, 32)
+    each(half, own_density, 64)
     if several:
         everything = pl.ds(1, devices - 1)
         whole = copy(outbox.at[everything], inbox.at[everything], 1)
@@ -268,9 +268,9 @@
             begin(s, 0, p_out, p_in)
 
         if s == 0:
-            each(local - half, lambda j: own_density(half + j), 32)
+            each(local - half, lambda j: own_density(half + j), 64)
         else:
-            each(local, own_density, 32)
+            each(local, own_density, 64)
         if domains > 1:
             finish(s, 0, p_out, p_in)
 
@@ -303,15 +303,16 @@
             pair_m[i, :, 0:256] = h
             pair_m[i, :, 256:512] = l
 
-        each(local, pair_density, 32)
+        each(local, pair_density, 64)
         chosen = jnp.concatenate([pair_row[s, 0:1], pair_row[s, 1:2]], 1)
         sent = send_row[s : s + 1, :]
         for side in range(2):
             r_out[s, side] = routed_sum(chosen, local + side * GHOSTS, GHOSTS, r_pair[...])
         for part in range(0, local, 128):
             r_own[part : part + 128] += routed_sum(chosen, part, 128, r_pair[...])
-        if domains > 1:
-            begin(s, 1, r_out, r_in)
+            if part == 0 and domains > 1:
+                begin(s, 1, r_out, r_in)
+        if domains > 1:
             finish(s, 1, r_out, r_in)
         incoming = jnp.concatenate([r_in[s, 0], r_in[s, 1]], 0)
         rho = (r_own[...] + routed_sum(sent, 0, local, incoming)) / masses[...]
@@ -336,7 +337,7 @@
             )
             f_own[pl.ds(i, 1), :] = lanes(force_rows(v, y))
 
-        each(local, own_force, 32)
+        each(local, own_force, 64)
         if domains > 1:
             finish(s, 2, q_out, q_in)
         press[local : local + GHOSTS] = q_in[s, 0]
@@ -363,13 +364,14 @@
             f_pair[pl.ds(i, 1), :] = lanes(force_rows(vs[1], down[:, :128]))
             f_pair[pl.ds(local + i, 1), :] = lanes(force_rows(vs[2], down[:, 128:]))
 
-        each(local, pair_force, 32)
+        each(local, pair_force, 64)
         for side in range(2):
             f_out[s, side] = routed_sum(chosen, local + side * GHOSTS, GHOSTS, f_pair[...])
         for part in range(0, local, 128):
             f_own[part : part + 128] += routed_sum(chosen, part, 128, f_pair[...])
-        if domains > 1:
-            begin(s, 3, f_out, f_in)
+            if part == 0 and domains > 1:
+                begin(s, 3, f_out, f_in)
+        if domains > 1:
             finish(s, 3, f_out, f_in)
         incoming = jnp.concatenate([f_in[s, 0], f_in[s, 1]], 0)
         for part in range(0, local, 128):

time: 134 us -> 127 us (0.948)
  Pallas kernels: 126 us -> 120 us
    pallas_call x1, Pallas kernels: 126 us -> 120 us  [run_steps(): pl.pallas_call(functools.partial(step_kernel, domains, subs, steps), name...]
where the time goes in v5:
time: 127 us
  Pallas kernels  120 us (94%)
  local copies, waits for them, and re-layouts  4.63 us (4%)
  other arithmetic  1.98 us (2%)
    pallas_call x1, Pallas kernels, run_steps(): pl.pallas_call(functools.partial(step_kernel, domains, subs, steps), name...  120 us
    unnamed x8, local copies, waits for them, and re-layouts  3.98 us

profile of v5, /device:TPU:8, one launch (start us, length us, event | category | flops | bytes accessed | tf_op | source)
XLA Modules:
  0.0 126.9 jit_solution(7721434701012260806)
XLA Ops:
  0.7 0.0 copy-start.1
  0.7 0.7 copy-done.1
  1.3 0.1 convert_reduce_fusion
  1.5 0.0 copy-start.2
  1.5 0.6 copy-done.2
  2.0 0.0 slice-start
  2.1 0.6 slice-done
  2.7 0.2 convert_reduce_fusion.1
  2.9 0.7 select_reduce_fusion.pack_index
  3.6 0.1 select_reduce_fusion.4
  3.7 0.1 select_reduce_fusion.3
  3.8 0.1 select_reduce_fusion.2
  4.0 0.6 pad_add_fusion.place_index
  4.6 119.6 %steps.1 = (f32[6,256,128]{2,1,0:T(8,128)}, f32[256,128]{1,0:T(8,128)}) custom-call(s32[256]{0:T(256)} %select_reduce_fusion.pack_index, s32[256]{0:T(256)} %pad_add_fusion.place_index, s32[2,128]{1,0:T(2,128)} %send_row.1, s32[2,2,256]{2,1,0:T(2,128)} %bitcast.5, s32[2,128]{1,0:T(2,128)} %send_row.1, s32[2,2,256]{2,1,0:T(2,128)} %bitcast.6, ...), custom_call_target="tpu_custom_call" | custom-call | tf_op jit(solution)/shard_map/steps/pallas_call | solution.py:405
  124.1 0.0 copy-start
  124.2 2.1 %copy.10 = f32[256,6,128]{2,0,1:T(8,128)} copy(f32[256,6,128]{2,0,1:T(8,128)} %bitcast.3) | data formatting | bytes 1572864
  126.3 0.0 copy-done
  126.3 0.7 copy.11
  (9 shorter events, 0.1 us)
Async XLA Ops:
  0.7 0.7 copy-start.1
  1.5 0.6 copy-start.2
  2.0 0.7 slice-start
  124.1 2.1 %copy-start = (f32[256,128]{1,0:T(8,128)S(1)}, f32[256,128]{1,0:T(8,128)}, u32[]{:S(2)}) copy-start(f32[256,128]{1,0:T(8,128)} %get-tuple-element.16) | copy-start | bytes 393220

commit v6 on v5

--- a/solution.py
+++ b/solution.py
@@ -112,10 +112,46 @@
     return out[:, :width] + out[:, width : 2 * width] + out[:, 2 * width :]
 
 
+def slot_numbers(me, devices, chosen):
+    local = chosen.shape[1]
+
+    def down(x):
+        return jnp.broadcast_to(x, (128, x.shape[1])).T
+
+    def count(hit, value):
+        return jnp.sum(jnp.where(hit, value, 0), axis=0, keepdims=True)
+
+    def number(shape, axis):
+        return lax.broadcasted_iota(jnp.int32, shape, axis)
+
+    wide, tall, square = (local, local), (local, 128), (128, 128)
+    column = down(chosen)
+    same = jnp.concatenate([column] * (local // 128), 1) == chosen
+    rank = count(same & (number(wide, 0) < number(wide, 1)), 1)
+    stays = chosen == me
+    shift = lax.rem(chosen - me + devices, devices)
+    slot = jnp.where(stays, devices * MOST + rank, shift * MOST + rank)
+    slot_down, shift_down = down(slot), down(jnp.where(stays, 0, shift))
+    block, lane = number(tall, 0), number(tall, 1)
+    rows = [
+        count(slot_down == lane + first, block)
+        for first in range(0, devices * MOST + local - devices, 128)
+    ]
+    come = count((shift_down == lane) & (lane > 0), 1)
+    k, other = number(square, 1), number(square, 0)
+    source, other_source = (lax.rem(me - x + devices, devices) for x in (k, other))
+    before = count(other_source < source, down(come))
+    arrive = 0
+    for r in range(MOST):
+        place = down(jnp.where(come > r, before + r, -1))
+        arrive = arrive + count(place == k, other * MOST + r)
+    return rows + [arrive]
+
+
 def step_kernel(
-    domains, subs, steps, pack_index, place_index, send, pairs, send_row, pair_row,
+    domains, subs, steps, send, pairs, chosen_device, send_row, pair_row,
     pos_vel, entropy_in, masses_in, final, density, outbox, inbox, state, blocks, press, entropy, masses, own_m, pair_m, r_own, r_pair, f_own, f_pair, f_sum,
-    p_out, p_in, r_out, r_in, q_out, q_in, f_out, f_in, send_sem, recv_sem, move_sems,
+    p_out, p_in, r_out, r_in, q_out, q_in, f_out, f_in, send_sem, recv_sem, move_sems, rows_out, index,
 ):
     local = state.shape[0]
     half = local // 2
@@ -173,6 +209,9 @@
 
         lax.fori_loop(1, devices, greet, 0)
 
+    for r, numbers in enumerate(slot_numbers(me, 128, chosen_device[...])):
+        rows_out[r : r + 1] = numbers
+
     packed = blocks
 
     def gather(g):
@@ -184,9 +223,17 @@
 
     each(local // 8, gather, 4)
 
+    to_scalars = pltpu.make_async_copy(rows_out, index, move_sems.at[2])
+    to_scalars.start()
+    to_scalars.wait()
+    slots = 128 * MOST
+
+    def number(t):
+        return index[t // 128, lax.rem(t, 128)]
+
     def pack(k):
         for r in range(MOST):
-            outbox[k, r] = packed[pack_index[k * MOST + r]]
+            outbox[k, r] = packed[number(k * MOST + r)]
 
     each(devices, pack)
 
@@ -222,12 +269,14 @@
         entropy[pl.ds(i, 1), :] = block[6:7]
         masses[pl.ds(i, 1), :] = block[7:8]
 
-    def scaled(i):
-        block = state[i]
-        level = jnp.log2(block[7:8])
-        blocks[i] = jnp.concatenate(
-            [block[0:3] * SCALE, level, level, jnp.zeros((3, 128), f32)], 0
-        )
+    def scaled(g):
+        rows = pl.ds(pl.multiple_of(g * 8, 8), 8)
+        level = jnp.log2(masses[rows, :])
+        for c in range(3):
+            blocks[rows, c, :] = state[rows, c, :] * SCALE
+            blocks[rows, 5 + c, :] = jnp.zeros((8, 128), f32)
+        blocks[rows, 3, :] = level
+        blocks[rows, 4, :] = level
 
     def own_density(i):
         block = blocks[i]
@@ -238,8 +287,8 @@
         own_m[i, 0:128] = h
         own_m[i, 128:256] = l
 
-    each(half, lambda j: enter(j, packed[place_index[j]]))
-    each(half, scaled)
+    each(half, lambda j: enter(j, packed[number(slots + j)]))
+    each(half // 8, scaled, 4)
     each(half, own_density, 64)
     if several:
         everything = pl.ds(1, devices - 1)
@@ -248,16 +297,16 @@
         whole.wait_recv()
 
     def come(j):
-        slot = place_index[half + j]
+        slot = number(slots + half + j)
         enter(half + j, inbox[slot // MOST, lax.rem(slot, MOST)])
-        scaled(half + j)
 
     each(half, come)
+    each(half // 8, lambda g: scaled(half // 8 + g), 4)
 
     for s in range(steps):
 
         if s > 0:
-            each(local, scaled)
+            each(local // 8, scaled, 4)
 
         def pick(j):
             for side in range(2):
@@ -377,23 +426,23 @@
         for part in range(0, local, 128):
             f_sum[part : part + 128] = f_own[part : part + 128] + routed_sum(sent, part, 128, incoming)
 
-        def move(i):
-            block = state[i]
-            push = f_sum[pl.ds(i, 1), :] * (STEP / SCALE)
-            push = jnp.concatenate([push[:, 0:128], push[:, 128:256], push[:, 256:384]], 0)
-            velocity = block[3:6] + push / block[7:8]
-            position = block[0:3] + STEP * velocity
-            if s == steps - 1:
-                for c in range(3):
-                    final[c, pl.ds(i, 1), :] = position[c : c + 1]
-                    final[3 + c, pl.ds(i, 1), :] = velocity[c : c + 1]
-            else:
-                state[i] = jnp.concatenate([position, velocity, block[6:8]], 0)
-
-        each(local, move)
-
-
-def run_steps(domains, subs, pack_index, place_index, send, pairs, pos_vel, entropy, masses):
+        def move(g):
+            rows = pl.ds(pl.multiple_of(g * 8, 8), 8)
+            gain = (STEP / SCALE) / masses[rows, :]
+            for c in range(3):
+                velocity = state[rows, 3 + c, :] + f_sum[rows, c * 128 : c * 128 + 128] * gain
+                position = state[rows, c, :] + STEP * velocity
+                if s == steps - 1:
+                    final[c, rows, :] = position
+                    final[3 + c, rows, :] = velocity
+                else:
+                    state[rows, c, :] = position
+                    state[rows, 3 + c, :] = velocity
+
+        each(local // 8, move, 4)
+
+
+def run_steps(domains, subs, chosen, send, pairs, pos_vel, entropy, masses):
     steps = send.shape[0]
     local = pos_vel.shape[1]
     devices = domains * subs
@@ -409,7 +458,7 @@
             jax.ShapeDtypeStruct((6, local, 128), f32),
             jax.ShapeDtypeStruct((local, 128), f32),
         ],
-        in_specs=[smem] * 4 + [vmem] * 5,
+        in_specs=[smem] * 2 + [vmem] * 6,
         out_specs=[vmem, vmem],
         scratch_shapes=[
             pltpu.VMEM((devices, MOST, 8, 128), f32),
@@ -429,45 +478,20 @@
             *buffers,
             pltpu.SemaphoreType.DMA((steps, 4, 2)),
             pltpu.SemaphoreType.DMA((steps, 4, 2)),
-            pltpu.SemaphoreType.DMA((2,)),
+            pltpu.SemaphoreType.DMA((3,)),
+            pltpu.VMEM((4, 128), jnp.int32),
+            pltpu.SMEM((4, 128), jnp.int32),
         ],
         compiler_params=pltpu.CompilerParams(
             vmem_limit_bytes=67_000_000,
             **(dict(collective_id=1, has_side_effects=True) if devices > 1 else {}),
         ),
-    )(pack_index, place_index, send, pairs, send, pairs, pos_vel, entropy, masses)
+    )(send, pairs, chosen, send, pairs, pos_vel, entropy, masses)
 
 
 def shards(pos_vel, entropy, masses, destination, ghost_send, pair_list):
-    devices = lax.axis_size(("dom", "sub"))
-    me = lax.axis_index(("dom", "sub"))
-    local = pos_vel.shape[0]
-    number = jnp.arange(local, dtype=jnp.int32)
-    device = jnp.arange(devices, dtype=jnp.int32)
-    slot = jnp.arange(devices * MOST, dtype=jnp.int32)
-    same = destination[:, None] == destination[None, :]
-    rank = jnp.sum((same & (number[:, None] < number[None, :])).astype(jnp.int32), 0)
-    staying = destination == me
-    shift = (destination - me) % devices
-    out_slot = jnp.where(staying, -1, shift * MOST + rank)
-    pack_index = jnp.sum(jnp.where(out_slot[:, None] == slot[None, :], number[:, None], 0), 0)
-    source = (me - device) % devices
-    come = jnp.sum((shift[:, None] == device[None, :]).astype(jnp.int32), 0)
-    come = jnp.where(device == 0, 0, come)
-    before = jnp.sum(jnp.where(source[:, None] < source[None, :], come[:, None], 0), 0)
-    half = local - devices
-    stay_index = jnp.sum(
-        jnp.where(staying[:, None] & (rank[:, None] == number[None, :half]), number[:, None], 0), 0
-    )
-    come_index = sum(
-        jnp.sum(
-            jnp.where((before[:, None] + r == device[None, :]) & (come[:, None] > r), device[:, None] * MOST + r, 0), 0
-        )
-        for r in range(MOST)
-    )
-    place_index = jnp.concatenate([stay_index, come_index])
     final, density = run_steps(
-        lax.axis_size("dom"), lax.axis_size("sub"), pack_index, place_index, ghost_send,
+        lax.axis_size("dom"), lax.axis_size("sub"), destination[None, :], ghost_send,
         jnp.transpose(pair_list, (0, 2, 1)), jnp.transpose(pos_vel, (1, 0, 2)), entropy, masses,
     )
     return jnp.transpose(final, (1, 0, 2)), density

time: 127 us -> 124 us (0.976)
  other arithmetic: 1.98 us -> 0 us
  local copies, waits for them, and re-layouts: 4.63 us -> 2.76 us
    reduce_sum x6 -> x0, other arithmetic: 1.35 us -> none  [the longest x1 0.68 us: shards(): jnp.sum(jnp.where(out_slot[:, None] == slot[None, :], number[:, None], 0)...]
    unnamed x8 -> x4, local copies, waits for them, and re-layouts: 3.98 us -> 2.76 us
where the time goes in v6:
time: 124 us
  Pallas kernels  120 us (97%)
  local copies, waits for them, and re-layouts  2.76 us (2%)
    pallas_call x1, Pallas kernels, run_steps(): pl.pallas_call(functools.partial(step_kernel, domains, subs, steps), name...  120 us
    unnamed x4, local copies, waits for them, and re-layouts  2.76 us

profile of v6, /device:TPU:8, one launch (start us, length us, event | category | flops | bytes accessed | tf_op | source)
XLA Modules:
  0.0 123.9 jit_solution(11222846612159504287)
XLA Ops:
  0.6 120.5 %steps.1 = (f32[6,256,128]{2,1,0:T(8,128)}, f32[256,128]{1,0:T(8,128)}) custom-call(s32[2,128]{1,0:T(2,128)} %send_row.1, s32[2,2,256]{2,1,0:T(2,128)} %bitcast.6, s32[1,256]{1,0:T(1,128)} %bitcast.8, s32[2,128]{1,0:T(2,128)} %send_row.1, s32[2,2,256]{2,1,0:T(2,128)} %bitcast.7, f32[6,256,128]{2,1,0:T(8,128)} %bitcast.4, f32[256,128]{1,0:T(8,128)} %entropy_in.1, ...), custom_call_target="tpu_custom_call" | custom-call | tf_op jit(solution)/shard_map/steps/pallas_call | solution.py:454
  121.1 0.0 copy-start
  121.1 2.1 %copy.10 = f32[256,6,128]{2,0,1:T(8,128)} copy(f32[256,6,128]{2,0,1:T(8,128)} %bitcast.5) | data formatting | bytes 1572864
  123.2 0.0 copy-done
  123.2 0.7 copy.11
Async XLA Ops:
  121.1 2.1 %copy-start = (f32[256,128]{1,0:T(8,128)S(1)}, f32[256,128]{1,0:T(8,128)}, u32[]{:S(2)}) copy-start(f32[256,128]{1,0:T(8,128)} %get-tuple-element.9) | copy-start | bytes 393220

commit v7 on v6

--- a/solution.py
+++ b/solution.py
@@ -431,12 +431,11 @@
             gain = (STEP / SCALE) / masses[rows, :]
             for c in range(3):
                 velocity = state[rows, 3 + c, :] + f_sum[rows, c * 128 : c * 128 + 128] * gain
-                position = state[rows, c, :] + STEP * velocity
                 if s == steps - 1:
-                    final[c, rows, :] = position
+                    final[c, rows, :] = state[rows, c, :]
                     final[3 + c, rows, :] = velocity
                 else:
-                    state[rows, c, :] = position
+                    state[rows, c, :] += STEP * velocity
                     state[rows, 3 + c, :] = velocity
 
         each(local // 8, move, 4)
@@ -494,7 +493,8 @@
         lax.axis_size("dom"), lax.axis_size("sub"), destination[None, :], ghost_send,
         jnp.transpose(pair_list, (0, 2, 1)), jnp.transpose(pos_vel, (1, 0, 2)), entropy, masses,
     )
-    return jnp.transpose(final, (1, 0, 2)), density
+    drift = lax.pad(final[3:], jnp.float32(0.0), ((0, 3, 0), (0, 0, 0), (0, 0, 0)))
+    return jnp.transpose(final + STEP * drift, (1, 0, 2)), density
 
 
 def solution(mesh):

time: 124 us -> 124 us (level)
    unnamed x4 -> x5, local copies, waits for them, and re-layouts: 2.76 us -> 0.8 us
where the time goes in v7:
time: 124 us
  Pallas kernels  120 us (97%)
  local copies, waits for them, and re-layouts  1.9 us (2%)
    pallas_call x1, Pallas kernels, run_steps(): pl.pallas_call(functools.partial(step_kernel, domains, subs, steps), name...  120 us

profile of v7, /device:TPU:8, one launch (start us, length us, event | category | flops | bytes accessed | tf_op | source)
XLA Modules:
  0.0 124.0 jit_solution(14251715061354514396)
XLA Ops:
  0.6 120.5 %steps.1 = (f32[6,256,128]{2,1,0:T(8,128)}, f32[256,128]{1,0:T(8,128)}) custom-call(s32[2,128]{1,0:T(2,128)} %send_row.1, s32[2,2,256]{2,1,0:T(2,128)} %bitcast.6, s32[1,256]{1,0:T(1,128)} %bitcast.8, s32[2,128]{1,0:T(2,128)} %send_row.1, s32[2,2,256]{2,1,0:T(2,128)} %bitcast.7, f32[6,256,128]{2,1,0:T(8,128)} %bitcast.5, f32[256,128]{1,0:T(8,128)} %entropy_in.1, ...), custom_call_target="tpu_custom_call" | custom-call | tf_op jit(solution)/shard_map/steps/pallas_call | solution.py:453
  121.1 0.0 copy-start
  121.1 1.1 slice.3
  122.2 0.1 copy-done
  122.4 0.0 copy-start.1
  122.4 0.9 add_bitcast_fusion
  123.3 0.0 copy-done.1
  123.3 0.7 copy.9
Async XLA Ops:
  121.1 1.3 %copy-start = (f32[6,256,128]{2,1,0:T(8,128)S(1)}, f32[6,256,128]{2,1,0:T(8,128)}, u32[]{:S(2)}) copy-start(f32[6,256,128]{2,1,0:T(8,128)} %get-tuple-element.4) | copy-start | bytes 2359300
  122.4 1.0 copy-start.1
